TPU v7x, 256 devices: a whole 4x4x8 slice. The times are simulated.
256 devices in a mesh: wide: 32 (over y, x, core), narrow: 8 (over z).
Axes of the slice: x: 4, y: 4, z: 8, core: 2. Of those that a mesh axis runs over, the one named last changes fastest.
Arguments:
- covariates: bfloat16 [524288, 128], P(('wide', 'narrow')), may hold values from -6 to 6
- level_codes: int32 [524288], P(('wide', 'narrow')), may hold values from 0 to 3
- sign_bits: int32 [524288], P(('wide', 'narrow')), may hold values from 0 to 1
- sample_rows: int32 [1024], P(('wide', 'narrow')), may hold values from 0 to 2047, as said below
- effects: float32 [512], replicated, may hold values from -6 to 6
- noise: float32 [524288], P(('wide', 'narrow')), may hold values from -8 to 8
Outputs:
- coefficients: float32 [512], replicated
- residual: float32 [524288], P(('wide', 'narrow'))
- factor: float32 [512, 512], replicated
Inputs may be any that keep to these rules, and one draw needn't show every extreme that they name: `sample_rows`: a local row offset on the device that owns the entry.
All inputs are finite; a program needn't handle non-finite values.
Results may differ from a plain program's by a relative error of at most 0.0006.
The roundings to bfloat16 on the way count: a program that leaves them out, or rounds other values in their place, can miss the bound.
Values may be sent and summed in bfloat16 or wider, within the bound.
A program may use at most 64 MiB of HBM per device.

v0:
```python
import math

import jax
import jax.numpy as jnp
from jax import lax
from jax.sharding import PartitionSpec as P

COV = 128
LEVELS = 4
HB = 256
SKETCH = 1024
ITERS = 4


half_root = math.sqrt(0.5)


def partner(value, axis, apart):
    mask = 2**apart
    pairs = [(source, source ^ mask) for source in range(lax.axis_size(axis))]
    return lax.ppermute(value, axis, pairs)


def hadamard(size):
    left = jnp.arange(size, dtype=jnp.int32)[:, None]
    right = jnp.arange(size, dtype=jnp.int32)[None, :]
    common = jnp.bitwise_and(left, right)
    parity = jnp.zeros((size, size), jnp.int32)
    for place in range(size.bit_length()):
        parity = parity + jnp.bitwise_and(jnp.right_shift(common, place), 1)
    return (1 - 2 * (parity % 2)).astype(jnp.bfloat16)


def tri_solve(lower, vector, transpose):
    return lax.linalg.triangular_solve(
        lower, vector[:, None], left_side=True, lower=True, transpose_a=transpose
    )[:, 0]


def combine_pair(own, theirs, upper):
    own_wide = own.astype(jnp.float32)
    their_wide = theirs.astype(jnp.float32)
    low = jnp.where(upper, their_wide, own_wide)
    high = jnp.where(upper, own_wide, their_wide)
    return (jnp.where(upper, low - high, low + high) * half_root).astype(jnp.bfloat16)


def body(covariates, level_codes, sign_bits, sample_rows, effects, noise):
    rows_dev = covariates.shape[0]
    cols = LEVELS * COV
    onehot = (level_codes[:, None] == jnp.arange(LEVELS, dtype=jnp.int32)[None, :]).astype(
        jnp.float32
    )
    flipped = covariates * (1 - 2 * sign_bits).astype(jnp.bfloat16)[:, None]
    design = (onehot.astype(jnp.bfloat16)[:, :, None] * flipped[:, None, :]).reshape(
        rows_dev // HB, HB, cols
    )
    local = jnp.einsum("ij,gjc->gic", hadamard(HB), design, preferred_element_type=jnp.float32)
    local = (local * (1.0 / math.sqrt(HB))).astype(jnp.bfloat16).reshape(rows_dev, cols)
    wide_index = lax.axis_index("wide")
    mixed = local
    for place in range(3):
        upper = jnp.bitwise_and(jnp.right_shift(wide_index, place), 1) == 1
        theirs = partner(mixed, "wide", place)
        mixed = combine_pair(mixed, theirs, upper)
    sketch = mixed[sample_rows]
    gram = lax.psum(
        jnp.dot(sketch.T, sketch, preferred_element_type=jnp.float32), ("wide", "narrow")
    )
    lower = jnp.linalg.cholesky(gram)
    factor = lower.T * math.sqrt(LEVELS / SKETCH)
    wide_cov = covariates.astype(jnp.float32)

    def apply_design(vector):
        values = jnp.dot(wide_cov, vector.reshape(LEVELS, COV).T, precision=lax.Precision.HIGHEST)
        return jnp.sum(values * onehot, axis=1)

    def adjoint(vector):
        return jnp.dot(
            (onehot * vector[:, None]).T, wide_cov, precision=lax.Precision.HIGHEST
        ).reshape(cols)

    resid = apply_design(effects) + noise
    gradient_now = lax.psum(adjoint(resid), ("wide", "narrow"))
    steer = tri_solve(lower, gradient_now, False)
    direction = steer
    gamma = jnp.sum(steer * steer)
    solved = jnp.zeros((cols,), jnp.float32)
    for step in range(ITERS):
        image = apply_design(tri_solve(lower, direction, True))
        alpha = gamma / lax.psum(jnp.sum(image * image), ("wide", "narrow"))
        solved = solved + alpha * direction
        resid = resid - alpha * image
        gradient_now = lax.psum(adjoint(resid), ("wide", "narrow"))
        steer = tri_solve(lower, gradient_now, False)
        gamma_new = jnp.sum(steer * steer)
        direction = steer + gamma_new / gamma * direction
        gamma = gamma_new
    return (tri_solve(lower, solved, True), resid, factor)


def solution(mesh):
    return jax.shard_map(
        body,
        mesh=mesh,
        in_specs=(
            P(("wide", "narrow"), None),
            P(("wide", "narrow")),
            P(("wide", "narrow")),
            P(("wide", "narrow")),
            P(),
            P(("wide", "narrow")),
        ),
        out_specs=(P(), P(("wide", "narrow")), P()),
        check_vma=False,
    )
```

profile of v0, /device:TPU:1, one launch (start us, length us, event | category | flops | bytes accessed | tf_op | source)
XLA Modules:
  0.0 1097.9 jit_solution(14000195256907005070)
XLA Ops:
  10.4 7.2 broadcast_multiply_fusion
  25.7 3.9 collective-permute-done
  29.6 4.1 multiply_convert_fusion.2
  33.8 47.2 %collective-permute-done.1 = bf16[2048,512]{1,0:T(8,128)(2,1)} collective-permute-done((bf16[2048,512]{1,0:T(8,128)(2,1)}, bf16[2048,512]{1,0:T(8,128)(2,1)}, u32[]{:S(2)}, u32[]{:S(2)}) %collective-permute-start.1) | collective-permute-done | bytes 2097184 | tf_op jit(solution)/shard_map/ppermute | solution.py:21
  85.4 46.5 %collective-permute-done.2 = bf16[2048,512]{1,0:T(8,128)(2,1)} collective-permute-done((bf16[2048,512]{1,0:T(8,128)(2,1)S(1)}, bf16[2048,512]{1,0:T(8,128)(2,1)}, u32[]{:S(2)}, u32[]{:S(2)}) %collective-permute-start.2) | collective-permute-done | bytes 2097184 | tf_op jit(solution)/shard_map/ppermute | solution.py:21
  131.9 4.1 multiply_convert_fusion
  140.7 79.7 %psum.64 = f32[512,1]{0,1:T(1,128)S(1)} all-reduce(f32[512,1]{0,1:T(1,128)S(1)} %bitcast.533), channel_id=1, replica_groups=mesh['wide'=32,'narrow'=8] {'wide','narrow'}, use_global_device_ids=true, to_apply=%region_10.11 | all-reduce | flops 512 | bytes 4096 | tf_op jit(solution)/shard_map/psum | solution.py:84
  220.5 176.9 %all-reduce.3.cloned.1.call-done = f32[512,512]{0,1:T(8,128)} async-done(((f32[512,512]{0,1:T(8,128)}), f32[512,512]{0,1:T(8,128)}) %all-reduce.3.cloned.1.call-update) | async-done | bytes 1048592 | tf_op jit(solution)/shard_map/psum | solution.py:67
  401.1 11.7 %cholesky.104 = f32[128,128]{1,0:T(8,128)S(1)} custom-call(f32[128,128]{1,0:T(8,128)S(1)} %cholesky.266), custom_call_target="Cholesky" | custom-call | tf_op jit(solution)/shard_map/jit(cholesky)/cholesky | solution.py:70
  412.8 9.8 custom-call.33
  425.3 11.7 %cholesky.217 = f32[128,128]{1,0:T(8,128)S(1)} custom-call(f32[128,128]{1,0:T(8,128)S(1)} %cholesky.270), custom_call_target="Cholesky" | custom-call | tf_op jit(solution)/shard_map/jit(cholesky)/cholesky | solution.py:70
  437.1 10.0 custom-call.34
  448.6 11.7 %cholesky.238 = f32[128,128]{1,0:T(8,128)S(1)} custom-call(f32[128,128]{1,0:T(8,128)S(1)} %cholesky.275), custom_call_target="Cholesky" | custom-call | tf_op jit(solution)/shard_map/jit(cholesky)/cholesky | solution.py:70
  461.1 9.8 custom-call.35
  472.4 11.7 %cholesky.255 = f32[128,128]{1,0:T(8,128)S(1)} custom-call(f32[128,128]{1,0:T(8,128)S(1)} %convolution_subtract_fusion.2), custom_call_target="Cholesky" | custom-call | tf_op jit(solution)/shard_map/jit(cholesky)/cholesky | solution.py:70
  489.5 8.5 while.18
  497.9 39.3 %custom-call.51 = f32[4,128,128]{1,2,0:T(8,128)S(1)} custom-call(f32[4,128,128]{2,1,0:T(8,128)S(1)} %get-tuple-element.71), custom_call_target="InvertDiagBlocksLowerTriangular" | custom-call | tf_op jit(solution)/shard_map/triangular_solve/custom-call.8 | solution.py:35
  542.0 77.5 %psum.65 = f32[]{:T(128)} all-reduce(f32[]{:T(128)} %multiply_reduce_fusion.3), channel_id=1, replica_groups=mesh['wide'=32,'narrow'=8] {'wide','narrow'}, use_global_device_ids=true, to_apply=%region_14.17 | all-reduce | flops 1 | bytes 8 | tf_op jit(solution)/shard_map/psum | solution.py:91
  621.2 73.2 %psum.66 = f32[512,1]{0,1:T(1,128)S(1)} all-reduce(f32[512,1]{0,1:T(1,128)S(1)} %bitcast.534), channel_id=1, replica_groups=mesh['wide'=32,'narrow'=8] {'wide','narrow'}, use_global_device_ids=true, to_apply=%region_15.18 | all-reduce | flops 512 | bytes 4096 | tf_op jit(solution)/shard_map/psum | solution.py:94
  700.4 74.2 %psum.67 = f32[]{:T(128)} all-reduce(f32[]{:T(128)} %multiply_reduce_fusion.2), channel_id=1, replica_groups=mesh['wide'=32,'narrow'=8] {'wide','narrow'}, use_global_device_ids=true, to_apply=%region_19.22 | all-reduce | flops 1 | bytes 8 | tf_op jit(solution)/shard_map/psum | solution.py:91
  776.3 73.4 %psum.68 = f32[512,1]{0,1:T(1,128)S(1)} all-reduce(f32[512,1]{0,1:T(1,128)S(1)} %bitcast.535), channel_id=1, replica_groups=mesh['wide'=32,'narrow'=8] {'wide','narrow'}, use_global_device_ids=true, to_apply=%region_20.23 | all-reduce | flops 512 | bytes 4096 | tf_op jit(solution)/shard_map/psum | solution.py:94
  855.8 74.2 %psum.69 = f32[]{:T(128)} all-reduce(f32[]{:T(128)} %multiply_reduce_fusion.1), channel_id=1, replica_groups=mesh['wide'=32,'narrow'=8] {'wide','narrow'}, use_global_device_ids=true, to_apply=%region_24.27 | all-reduce | flops 1 | bytes 8 | tf_op jit(solution)/shard_map/psum | solution.py:91
  931.7 73.6 %psum.70 = f32[512,1]{0,1:T(1,128)S(1)} all-reduce(f32[512,1]{0,1:T(1,128)S(1)} %bitcast.536), channel_id=1, replica_groups=mesh['wide'=32,'narrow'=8] {'wide','narrow'}, use_global_device_ids=true, to_apply=%region_25.28 | all-reduce | flops 512 | bytes 4096 | tf_op jit(solution)/shard_map/psum | solution.py:94
  1011.3 74.1 %psum.71 = f32[]{:T(128)} all-reduce(f32[]{:T(128)} %multiply_reduce_fusion), channel_id=1, replica_groups=mesh['wide'=32,'narrow'=8] {'wide','narrow'}, use_global_device_ids=true, to_apply=%region_29.32 | all-reduce | flops 1 | bytes 8 | tf_op jit(solution)/shard_map/psum | solution.py:91
  (160 shorter events, 65.6 us)
Async XLA Ops:
  7.2 132.7 %copy-start = (f32[512]{0:T(512)S(1)}, f32[512]{0:T(512)}, u32[]{:S(2)}) copy-start(f32[512]{0:T(512)} %param.14) | copy-start | bytes 6148
  7.2 390.2 %all-reduce.3.cloned.1.call-start = ((), (), s32[]{:S(2)}) async-start(), calls=%async_computation | async-start | bytes 2097152 | tf_op jit(solution)/shard_map/psum | solution.py:67
  22.4 7.2 collective-permute-start
  33.8 47.2 %collective-permute-start.1 = (bf16[2048,512]{1,0:T(8,128)(2,1)}, bf16[2048,512]{1,0:T(8,128)(2,1)}, u32[]{:S(2)}, u32[]{:S(2)}) collective-permute-start(bf16[2048,512]{1,0:T(8,128)(2,1)} %multiply_convert_fusion.2), channel_id=1, source_target_pairs={{0,16},{8,24},{16,0},{24,8},{32,48},{40,56},{48,32},{56,40},{64,80... | collective-permute-start | bytes 6291464 | tf_op jit(solution)/shard_map/ppermute | solution.py:21
  33.8 51.7 %copy-start.6 = (s32[4]{0:T(128)S(1)}, s32[4]{0:T(128)}, u32[]{:S(2)}) copy-start(s32[4]{0:T(128)} %param.13) | copy-start | bytes 52
  84.3 47.6 %collective-permute-start.2 = (bf16[2048,512]{1,0:T(8,128)(2,1)S(1)}, bf16[2048,512]{1,0:T(8,128)(2,1)}, u32[]{:S(2)}, u32[]{:S(2)}) collective-permute-start(bf16[2048,512]{1,0:T(8,128)(2,1)S(1)} %multiply_convert_fusion.1), channel_id=1, source_target_pairs={{0,32},{8,40},{16,48},{24,56},{32,0},{40,8},{48,16},{56,24},{64,96... | collective-permute-start | bytes 6291464 | tf_op jit(solution)/shard_map/ppermute | solution.py:21
  136.0 3.9 copy-start.1
  136.0 3.9 copy-start.4
  136.0 4.4 copy-start.5
  397.4 1.7 copy-start.2
  850.3 237.1 %copy-start.3 = (f32[512,512]{0,1:T(8,128)S(1)}, f32[512,512]{0,1:T(8,128)}, u32[]{:S(2)}) copy-start(f32[512,512]{0,1:T(8,128)} %get-tuple-element.93) | copy-start | bytes 3145732
Sparse Core Ops, SparseCore 0:
  140.0 257.3 all-reduce.2
where the time goes:
time: 1110 us; the launch traced here: 1100 us
  blocking collectives  600 us (54%)
  waiting for transfers between devices  275 us (25%)
  other arithmetic  148 us (13%)
  between operations  26.6 us (2%)
  matrix products  26.4 us (2%)
  local copies, waits for them, and re-layouts  17.4 us (2%)
    psum x4, blocking collectives, body(): alpha = gamma / lax.psum(jnp.sum(image * image), ('wide', 'narrow'))  300 us
    psum x4, blocking collectives, body(): gradient_now = lax.psum(adjoint(resid), ('wide', 'narrow'))  300 us
    psum x1, waiting for transfers between devices, body(): lax.psum(jnp.dot(sketch.T, sketch, preferred_element_type=jnp.float32), (...  177 us
    ppermute x3, waiting for transfers between devices, partner(): return lax.ppermute(value, axis, pairs)  97.6 us
    another operation x14, other arithmetic, body(): lower = jnp.linalg.cholesky(gram)  78.6 us
    another operation x8, other arithmetic, tri_solve(): lax.linalg.triangular_solve(lower, vector[:, None], left_side=True, lower...  40 us
  transfers between devices with their start and end apart: 4, of which 4 were waited for; matrix products, arithmetic and copies ran while one was open for 0% of the time, Pallas kernels for 0%

commit v1 on v0

v1 whole, which is shorter than its diff:
```python
import functools
import math

import jax
import jax.numpy as jnp
from jax import lax
from jax.experimental import pallas as pl
from jax.experimental.pallas import tpu as pltpu
from jax.sharding import PartitionSpec as P

COV = 128
LEVELS = 4
COLS = COV * LEVELS
ROWS = 2048
HB = 256
SKETCH = 1024
SAMP = 4
ITERS = 4
GROUP = 8
NZ = 8
NXY = 16
EXTRA = 8
LANES = 128

HALF_ROOT = math.sqrt(0.5)
HIGH = lax.Precision.HIGHEST
MESH = pl.DeviceIdType.MESH
F32 = jnp.float32
BF16 = jnp.bfloat16


def iota(shape, axis):
    return lax.broadcasted_iota(jnp.int32, shape, axis)


def split3(value):
    high = value.astype(BF16)
    rest = value - high.astype(F32)
    middle = rest.astype(BF16)
    low = (rest - middle.astype(F32)).astype(BF16)
    return high.astype(F32), middle.astype(F32), low.astype(F32)


def gather_kernel(
    samp_ref, cov_ref, codes_ref, bits_ref, noise_ref,
    sketch_ref, square_ref, extra_ref,
    own, asked, picks, lhs, sent, held, rowz,
    halves, half_in, pieces, piece_in, plane, plane_in,
    send, recv,
):
    wide = lax.axis_index("wide")
    z = lax.axis_index("narrow")
    core = lax.rem(wide, 2)
    q = wide // 2
    member = lax.rem(wide, GROUP)
    base = wide - member
    sibling = wide + 1 - 2 * core

    def mix_peer(o):
        return lax.rem(member + o, GROUP)

    def z_peer(o):
        return lax.rem(z + o, NZ)

    def xy_peer(o):
        return lax.rem(q + o, NXY)

    slots = iter(range(200))

    def remote(src, dst, to_wide, to_z):
        slot = next(slots)
        return pltpu.make_async_remote_copy(
            src_ref=src, dst_ref=dst, send_sem=send.at[slot], recv_sem=recv.at[slot],
            device_id=(to_wide, to_z), device_id_type=MESH,
        )

    barrier = pltpu.get_barrier_semaphore()
    greeted = 0
    for o in range(1, GROUP):
        pl.semaphore_signal(barrier, inc=1, device_id=(base + mix_peer(o), z), device_id_type=MESH)
        greeted += 1
    for o in range(1, NZ):
        pl.semaphore_signal(barrier, inc=1, device_id=(wide, z_peer(o)), device_id_type=MESH)
        greeted += 1
    for o in range(1, NXY):
        pl.semaphore_signal(
            barrier, inc=1, device_id=(2 * xy_peer(o) + core, z), device_id_type=MESH
        )
        greeted += 1

    for k in range(8):
        own[k : k + 1, :] = jnp.full((1, LANES), samp_ref[k % SAMP], jnp.int32)
    asked[member] = own[...]
    pl.semaphore_wait(barrier, greeted)

    ask = [remote(own, asked.at[member], base + mix_peer(o), z) for o in range(1, GROUP)]
    for copy in ask:
        copy.start()

    codes = codes_ref[...]
    flip = cov_ref[...].astype(F32).T
    for level in range(LEVELS):
        mask = (codes == level).astype(F32)
        lhs[level * COV : (level + 1) * COV, :] = (flip * mask).astype(BF16)
    masks = [(codes == level).astype(F32) for level in range(LEVELS)]
    parts = split3(noise_ref[...])
    shadow_rows = [part * mask for part in parts for mask in masks]
    shadow_rows = jnp.concatenate(shadow_rows + [jnp.zeros((4, ROWS), F32)], axis=0)
    normal = jnp.dot(lhs[...], cov_ref[...], preferred_element_type=F32)
    shadow = jnp.dot(shadow_rows.astype(BF16), cov_ref[...], preferred_element_type=F32)
    shadow = shadow[0:4] + shadow[4:8] + shadow[8:12]
    sub = iota((COV, COV), 0)
    lane = iota((COV, COV), 1)
    squares = []
    diagonals = []
    for pair in range(2):
        even = normal[2 * pair * COV : (2 * pair + 1) * COV]
        odd = normal[(2 * pair + 1) * COV : (2 * pair + 2) * COV]
        halves[pair, 0:COV, :] = jnp.where(lane >= sub, even, odd)
        diagonals.append(jnp.sum(jnp.where(lane == sub, odd, 0.0), axis=0, keepdims=True))
    extra = jnp.concatenate([shadow] + diagonals + [jnp.zeros((2, COV), F32)], axis=0)
    halves[0, COV:, :] = extra
    halves[1, COV:, :] = extra
    a_core = remote(halves.at[1 - core], half_in, sibling, z)
    a_core.start()

    for copy in ask:
        copy.wait_recv()
    want = jnp.concatenate([asked[i] for i in range(GROUP)], axis=0)
    shape = (GROUP * 8, LANES)
    common = want & iota(shape, 1)
    common = common ^ (common >> 4)
    common = common ^ (common >> 2)
    low = common ^ (common >> 1)
    top = (want >> 7) & 1
    block = want >> 8
    for chunk in range(ROWS // LANES):
        span = slice(chunk * LANES, (chunk + 1) * LANES)
        parity = low ^ bits_ref[:, span]
        if chunk % 2:
            parity = parity ^ top
        sign = (1 - 2 * (parity & 1)).astype(F32)
        sign = jnp.where(block == chunk // 2, sign, 0.0)
        here = codes_ref[:, span]
        for level in range(LEVELS):
            value = sign * (here == level).astype(F32)
            picks[level * 64 : (level + 1) * 64, span] = value.astype(BF16)
    local = jnp.dot(picks[...], cov_ref[...], preferred_element_type=F32)
    local = local * (1.0 / math.sqrt(HB))
    local = jnp.concatenate([local[level * 64 : (level + 1) * 64] for level in range(LEVELS)], axis=1)
    for i in range(GROUP):
        sent[i] = local[i * 8 : i * 8 + SAMP].astype(BF16)
    held[member] = sent[member]
    rows = [
        remote(sent.at[mix_peer(o)], held.at[member], base + mix_peer(o), z)
        for o in range(1, GROUP)
    ]
    for copy in rows:
        copy.start()

    a_core.wait_recv()
    mine = halves[core] + half_in[...]
    for i in range(NZ):
        pieces[i] = jnp.concatenate([mine[i * 16 : (i + 1) * 16], mine[COV:]], axis=0)
    piece_in[z] = pieces[z]
    a_z = [
        remote(pieces.at[z_peer(o)], piece_in.at[z], wide, z_peer(o)) for o in range(1, NZ)
    ]

    for copy in rows:
        copy.wait_recv()
    level_rows = [held[i].astype(F32) for i in range(GROUP)]
    for place in range(3):
        side = (1 - 2 * lax.rem(wide // (2**place), 2)).astype(F32)
        level_rows = [
            ((level_rows[i] + side * level_rows[i + 1]) * HALF_ROOT).astype(BF16).astype(F32)
            for i in range(0, len(level_rows), 2)
        ]
    rowz[z] = level_rows[0].astype(BF16)
    s_z = [remote(rowz.at[z], rowz.at[z], wide, z_peer(o)) for o in range(1, NZ)]
    for copy in s_z:
        copy.start()
    for copy in a_z:
        copy.start()

    for copy in s_z:
        copy.wait_recv()
    stack = jnp.concatenate([rowz[i].astype(F32) for i in range(NZ)], axis=0)
    sketch_ref[core, q] = stack.astype(BF16)
    s_xy = [
        remote(sketch_ref.at[core, q], sketch_ref.at[core, q], 2 * xy_peer(o) + core, z)
        for o in range(1, NXY)
    ]
    for copy in s_xy:
        copy.start()
    s_core = [remote(sketch_ref.at[core, q], sketch_ref.at[core, q], sibling, z)]
    s_core[0].start()

    for copy in a_z:
        copy.wait_recv()
    total = piece_in[0]
    for i in range(1, NZ):
        total = total + piece_in[i]
    plane_in[q] = total
    a_xy = [
        remote(plane_in.at[q], plane_in.at[q], 2 * xy_peer(o) + core, z) for o in range(1, NXY)
    ]
    for copy in a_xy:
        copy.start()

    for o in range(1, NXY):
        s_xy[o - 1].wait_recv()
        from_q = lax.rem(q - o + NXY, NXY)
        copy = remote(sketch_ref.at[core, from_q], sketch_ref.at[core, from_q], sibling, z)
        copy.start()
        s_core.append(copy)

    for copy in a_xy:
        copy.wait_recv()
    total = plane_in[0]
    for i in range(1, NXY):
        total = total + plane_in[i]
    extra_ref[...] = total[16:]
    square_ref[core, z] = total[:16]
    a_out = [
        remote(square_ref.at[core, z], square_ref.at[core, z], wide, z_peer(o))
        for o in range(1, NZ)
    ]
    for copy in a_out:
        copy.start()
    for copy in a_out:
        copy.wait_recv()
    a_last = remote(square_ref.at[core], square_ref.at[core], sibling, z)
    a_last.start()
    a_last.wait_recv()
    for copy in s_core:
        copy.wait_recv()
    for copy in ask + [a_core] + rows + a_z + s_z + s_xy + a_xy + s_core + a_out + [a_last]:
        copy.wait_send()


N_COPIES = 3 * 7 + 1 + 7 + 1 + 15 + 15 + 15 + 7 + 1


def gather(samples, covariates, codes, bits, noise):
    vmem = pl.BlockSpec(memory_space=pltpu.VMEM)
    smem = pl.BlockSpec(memory_space=pltpu.SMEM)
    return pl.pallas_call(
        gather_kernel,
        out_shape=(
            jax.ShapeDtypeStruct((2, NXY, 32, COLS), BF16),
            jax.ShapeDtypeStruct((2, NZ, 16, COV), F32),
            jax.ShapeDtypeStruct((EXTRA, COV), F32),
        ),
        in_specs=[smem, vmem, vmem, vmem, vmem],
        out_specs=(vmem, vmem, vmem),
        scratch_shapes=[
            pltpu.VMEM((8, LANES), jnp.int32),
            pltpu.VMEM((GROUP, 8, LANES), jnp.int32),
            pltpu.VMEM((LEVELS * 64, ROWS), BF16),
            pltpu.VMEM((COLS, ROWS), BF16),
            pltpu.VMEM((GROUP, SAMP, COLS), BF16),
            pltpu.VMEM((GROUP, SAMP, COLS), BF16),
            pltpu.VMEM((NZ, SAMP, COLS), BF16),
            pltpu.VMEM((2, COV + EXTRA, COV), F32),
            pltpu.VMEM((COV + EXTRA, COV), F32),
            pltpu.VMEM((NZ, 16 + EXTRA, COV), F32),
            pltpu.VMEM((NZ, 16 + EXTRA, COV), F32),
            pltpu.VMEM((16 + EXTRA, COV), F32),
            pltpu.VMEM((NXY, 16 + EXTRA, COV), F32),
            pltpu.SemaphoreType.DMA((N_COPIES,)),
            pltpu.SemaphoreType.DMA((N_COPIES,)),
        ],
        compiler_params=pltpu.CompilerParams(
            collective_id=0, has_side_effects=True, vmem_limit_bytes=40 << 20
        ),
        name="gather_sketch",
    )(samples, covariates, codes, bits, noise)


def spread(value, index):
    return jnp.broadcast_to(value[index : index + 1, :], value.shape)


def invert_factor(matrix):
    count = COV // 8
    rows = [matrix[8 * t : 8 * t + 8, :] for t in range(count)]
    sub = iota((8, COV), 0)
    lane = iota((8, COV), 1)
    for p in range(count):
        first = 8 * p
        own = [
            [jnp.broadcast_to(rows[t][:, first + i : first + i + 1], (8, COV)) for t in range(p, count)]
            for i in range(8)
        ]
        panel = (lane >= first) & (lane < first + 8)
        for t in range(p + 1, count):
            rows[t] = jnp.where(panel, 0.0, rows[t])
        rows[p] = jnp.where(panel, jnp.where(lane == first + sub, 1.0, 0.0), rows[p])
        for i in range(8):
            root = lax.rsqrt(spread(own[i][0], i))
            row = spread(rows[p], i) * root
            upper = {k: spread(own[k][0], i) * root for k in range(i + 1, 8)}
            for t in range(p, count):
                scale = own[i][t - p] * root
                if t == p:
                    scale = jnp.where(sub > i, scale, 0.0)
                    rows[t] = jnp.where(sub == i, row, rows[t] - scale * row)
                else:
                    rows[t] = rows[t] - scale * row
                for k in range(i + 1, 8):
                    own[k][t - p] = own[k][t - p] - scale * upper[k]
    for p in range(count):
        rows[p] = jnp.where(lane <= 8 * p + sub, rows[p], 0.0)
    return jnp.concatenate(rows, axis=0)


def blk(index):
    return slice(index * COV, (index + 1) * COV)


def solve_kernel(
    sketch_ref, square_ref, extra_ref, effects_ref, cov_ref, codes_ref, noise_ref,
    coef_ref, resid_ref, factor_ref, gram, inverse,
):
    n = LEVELS
    sub = iota((COV, COV), 0)
    lane = iota((COV, COV), 1)
    scale = math.sqrt(LEVELS / SKETCH)
    for k in range(n):
        gram[k, :, k * COV :] = lax.dot_general(
            sketch_ref[:, blk(k)], sketch_ref[:, k * COV :], (((0,), (0,)), ((), ())),
            preferred_element_type=F32,
        )
    for k in range(n):
        corner = invert_factor(gram[k, :, blk(k)])
        inverse[k, :, blk(k)] = corner
        product = jnp.dot(corner, gram[k], precision=HIGH, preferred_element_type=F32)
        if k:
            inverse[k, :, : k * COV] = product[:, : k * COV]
            factor_ref[blk(k), : k * COV] = jnp.zeros((COV, k * COV), F32)
        factor_ref[blk(k), blk(k)] = jnp.where(lane >= sub, product[:, blk(k)], 0.0) * scale
        if k + 1 < n:
            factor_ref[blk(k), (k + 1) * COV :] = product[:, (k + 1) * COV :] * scale
        for i in range(k + 1, n):
            back = product[:, blk(i)].T
            change = jnp.dot(back, product[:, i * COV :], precision=HIGH, preferred_element_type=F32)
            gram[i, :, i * COV :] = gram[i, :, i * COV :] - change
        for i in range(k + 1, n):
            back = product[:, blk(i)].T
            gram[i, :, blk(k)] = -jnp.dot(back, corner, precision=HIGH, preferred_element_type=F32)
            if k:
                change = jnp.dot(back, product[:, : k * COV], precision=HIGH, preferred_element_type=F32)
                gram[i, :, : k * COV] = gram[i, :, : k * COV] - change

    normal = []
    for pair in range(2):
        square = square_ref[pair]
        turned = square.T
        diagonal = extra_ref[4 + pair : 5 + pair, :]
        normal.append(jnp.where(lane >= sub, square, turned))
        normal.append(jnp.where(lane < sub, square, jnp.where(lane > sub, turned, diagonal)))

    def apply_normal(rows):
        out = []
        for level in range(n):
            column = jnp.sum(normal[level] * rows[level], axis=1, keepdims=True)
            out.append(jnp.sum(jnp.where(lane == sub, column, 0.0), axis=0, keepdims=True))
        return out

    def forward(rows):
        out = []
        for k in range(n):
            acc = inverse[k, :, blk(0)] * rows[0]
            for c in range(1, k + 1):
                acc = acc + inverse[k, :, blk(c)] * rows[c]
            out.append(jnp.sum(acc, axis=1, keepdims=True))
        return out

    def backward(columns):
        out = []
        for c in range(n):
            acc = inverse[c, :, blk(c)] * columns[c]
            for k in range(c + 1, n):
                acc = acc + inverse[k, :, blk(c)] * columns[k]
            out.append(jnp.sum(acc, axis=0, keepdims=True))
        return out

    def dot(left, right, axis):
        acc = left[0] * right[0]
        for a, b in zip(left[1:], right[1:]):
            acc = acc + a * b
        return jnp.sum(acc, axis=axis, keepdims=True)

    effects = [effects_ref[:, blk(level)] for level in range(n)]
    gradient = [
        image + extra_ref[level : level + 1, :] for level, image in enumerate(apply_normal(effects))
    ]
    steer = forward(gradient)
    gamma = dot(steer, steer, 0)
    direction = backward(steer)
    solved = [jnp.zeros((1, COV), F32)] * n
    for step in range(ITERS):
        image = apply_normal(direction)
        alpha = gamma / dot(direction, image, 1)
        solved = [a + alpha * b for a, b in zip(solved, direction)]
        if step + 1 < ITERS:
            gradient = [a - alpha * b for a, b in zip(gradient, image)]
            steer = forward(gradient)
            gamma_new = dot(steer, steer, 0)
            ratio = gamma_new / gamma
            direction = [a + ratio * b for a, b in zip(backward(steer), direction)]
            gamma = gamma_new
    left = []
    for level in range(n):
        coef_ref[:, blk(level)] = solved[level]
        left.append(effects[level] - solved[level])
    parts = split3(jnp.concatenate(left, axis=0))
    weights = jnp.concatenate(list(parts) + [jnp.zeros((4, COV), F32)], axis=0).astype(BF16)
    values = lax.dot_general(
        weights, cov_ref[...], (((1,), (1,)), ((), ())), preferred_element_type=F32
    )
    codes = codes_ref[...]
    resid = noise_ref[...]
    for level in range(n):
        value = values[level : level + 1] + values[4 + level : 5 + level] + values[8 + level : 9 + level]
        resid = resid + jnp.where(codes == level, value, 0.0)
    resid_ref[...] = resid


def solve(sketch, square, extra, effects, covariates, codes, noise):
    vmem = pl.BlockSpec(memory_space=pltpu.VMEM)
    return pl.pallas_call(
        solve_kernel,
        out_shape=(
            jax.ShapeDtypeStruct((1, COLS), F32),
            jax.ShapeDtypeStruct((1, ROWS), F32),
            jax.ShapeDtypeStruct((COLS, COLS), F32),
        ),
        in_specs=[vmem] * 7,
        out_specs=(vmem,) * 3,
        scratch_shapes=[
            pltpu.VMEM((LEVELS, COV, COLS), F32),
            pltpu.VMEM((LEVELS, COV, COLS), F32),
        ],
        compiler_params=pltpu.CompilerParams(vmem_limit_bytes=40 << 20),
        name="solve",
    )(sketch, square, extra, effects, covariates, codes, noise)


def body(covariates, level_codes, sign_bits, sample_rows, effects, noise):
    codes = level_codes.reshape(1, ROWS)
    noise = noise.reshape(1, ROWS)
    sketch, square, extra = gather(
        sample_rows, covariates, codes, sign_bits.reshape(1, ROWS), noise
    )
    coef, resid, factor = solve(
        sketch.reshape(SKETCH, COLS), square.reshape(2, COV, COV), extra,
        effects.reshape(1, COLS), covariates, codes, noise,
    )
    return coef.reshape(COLS), resid.reshape(ROWS), factor


def solution(mesh):
    rows = P(("wide", "narrow"))
    return jax.shard_map(
        body,
        mesh=mesh,
        in_specs=(P(("wide", "narrow"), None), rows, rows, rows, P(), rows),
        out_specs=(P(), rows, P()),
        check_vma=False,
    )
```

time: 1110 us -> 69.7 us (0.06); the launches traced: 1100 us -> 69.3 us
  blocking collectives: 600 us -> 0 us
  waiting for transfers between devices: 275 us -> 0 us
  other arithmetic: 148 us -> 0 us
  Pallas kernels: 0 us -> 64.2 us
  matrix products: 26.4 us -> 0 us
  between operations: 26.6 us -> 0.68 us
  local copies, waits for them, and re-layouts: 17.4 us -> 4.46 us
    psum x8 -> x0, blocking collectives: 600 us -> none  [the longest x4 300 us: body(): alpha = gamma / lax.psum(jnp.sum(image * image), ('wide', 'narrow'))]
    psum x1 -> x0, waiting for transfers between devices: 177 us -> none  [body(): lax.psum(jnp.dot(sketch.T, sketch, preferred_element_type=jnp.float32), (...]
    another operation x22 -> x0, other arithmetic: 119 us -> none  [the longest x14 78.6 us: body(): lower = jnp.linalg.cholesky(gram)]
    ppermute x3 -> x0, waiting for transfers between devices: 97.6 us -> none  [partner(): return lax.ppermute(value, axis, pairs)]
    pallas_call x0 -> x2, Pallas kernels: none -> 64.2 us  [the longest x1 42 us: gather(): pl.pallas_call(gather_kernel, out_shape=(jax.ShapeDtypeStruct((2, NXY, 32...]
    another operation x69 -> x0, matrix products: 18.5 us -> none  [the longest x63 13 us: tri_solve(): lax.linalg.triangular_solve(lower, vector[:, None], left_side=True, lower...]
    convert_element_type x5 -> x0, other arithmetic: 13 us -> none  [the longest x3 11.6 us: combine_pair(): (jnp.where(upper, low - high, low + high) * half_root).astype(jnp.bfloat16)]
  transfers between devices with their start and end apart: 4 -> 0, of which waited for: 4 -> 0; matrix products, arithmetic and copies ran while one was open for 0% -> 0% of each run, Pallas kernels for 0% -> 0%
where the time goes in v1:
time: 69.7 us; the launch traced here: 69.3 us
  Pallas kernels  64.2 us (92%)
  local copies, waits for them, and re-layouts  4.46 us (6%)
    pallas_call x1, Pallas kernels, gather(): pl.pallas_call(gather_kernel, out_shape=(jax.ShapeDtypeStruct((2, NXY, 32...  42 us
    pallas_call x1, Pallas kernels, solve(): pl.pallas_call(solve_kernel, out_shape=(jax.ShapeDtypeStruct((1, COLS), F...  22.3 us
    unnamed x16, local copies, waits for them, and re-layouts  4.46 us

profile of v1, /device:TPU:1, one launch (start us, length us, event | category | flops | bytes accessed | tf_op | source)
XLA Modules:
  0.0 69.3 jit_solution(4629210792317730794)
XLA Ops:
  0.6 0.0 copy-start.7
  0.6 0.6 copy-done.7
  1.3 0.0 copy-start
  1.3 1.0 %copy-done = bf16[2048,128]{1,0:T(8,128)(2,1)S(1)} copy-done((bf16[2048,128]{1,0:T(8,128)(2,1)S(1)}, bf16[2048,128]{1,0:T(8,128)(2,1)}, u32[]{:S(2)}) %copy-start) | copy-done | bytes 524312
  2.3 0.0 copy-start.2
  2.3 0.7 %copy-done.2 = s32[2048]{0:T(1024)S(1)} copy-done((s32[2048]{0:T(1024)S(1)}, s32[2048]{0:T(1024)}, u32[]{:S(2)}) %copy-start.2) | copy-done | bytes 8216
  3.0 0.0 copy-start.4
  3.0 0.7 %copy-done.4 = f32[2048]{0:T(1024)S(1)} copy-done((f32[2048]{0:T(1024)S(1)}, f32[2048]{0:T(1024)}, u32[]{:S(2)}) %copy-start.4) | copy-done | bytes 8216
  3.7 0.0 copy-start.5
  3.7 0.7 %copy-done.5 = s32[2048]{0:T(1024)S(1)} copy-done((s32[2048]{0:T(1024)S(1)}, s32[2048]{0:T(1024)}, u32[]{:S(2)}) %copy-start.5) | copy-done | bytes 8216
  4.4 0.0 copy-start.1
  4.4 0.0 copy-start.6
  4.4 42.0 %gather_sketch.1 = (bf16[2,16,32,512]{3,2,1,0:T(8,128)(2,1)S(1)}, f32[2,8,16,128]{3,2,1,0:T(8,128)S(1)}, f32[8,128]{1,0:T(8,128)S(1)}) custom-call(s32[4]{0:T(128)S(1)} %copy-done.7, bf16[2048,128]{1,0:T(8,128)(2,1)S(1)} %copy-done, s32[1,2048]{1,0:T(1,128)S(1)} %bitcast.10, s32[1,2048]{1,0:T(1,128)S(1)} %bitcast.14, f32[1,2048]{1,0:T(1,128)S(1)} %bitcast.12), custom_call_target="tpu_custom_call" | custom-call | tf_op jit(solution)/shard_map/gather_sketch/pallas_call | solution.py:248
  46.4 0.0 copy-start.3
  46.4 0.0 copy-done.1
  46.4 0.0 copy-done.6
  46.4 0.7 copy-done.3
  47.1 22.3 %solve.1 = (f32[1,512]{1,0:T(1,128)}, f32[1,2048]{1,0:T(1,128)}, f32[512,512]{1,0:T(8,128)}) custom-call(bf16[1024,512]{1,0:T(8,128)(2,1)S(1)} %bitcast.8, f32[2,128,128]{2,1,0:T(8,128)S(1)} %bitcast.9, f32[8,128]{1,0:T(8,128)S(1)} %get-tuple-element.11.extra_ref, f32[1,512]{1,0:T(1,128)S(1)} %bitcast.15, bf16[2048,128]{1,0:T(8,128)(2,1)S(1)} %copy-done.1, ...), custom_call_target="tpu_custom_call" | custom-call | tf_op jit(solution)/shard_map/solve/pallas_call | solution.py:433
Async XLA Ops:
  0.6 0.7 copy-start.7
  1.3 1.0 %copy-start = (bf16[2048,128]{1,0:T(8,128)(2,1)S(1)}, bf16[2048,128]{1,0:T(8,128)(2,1)}, u32[]{:S(2)}) copy-start(bf16[2048,128]{1,0:T(8,128)(2,1)} %cov_ref.3) | copy-start | bytes 1572868
  2.3 0.7 %copy-start.2 = (s32[2048]{0:T(1024)S(1)}, s32[2048]{0:T(1024)}, u32[]{:S(2)}) copy-start(s32[2048]{0:T(1024)} %param.7) | copy-start | bytes 24580
  3.0 0.7 %copy-start.4 = (f32[2048]{0:T(1024)S(1)}, f32[2048]{0:T(1024)}, u32[]{:S(2)}) copy-start(f32[2048]{0:T(1024)} %param.11) | copy-start | bytes 24580
  3.7 0.7 %copy-start.5 = (s32[2048]{0:T(1024)S(1)}, s32[2048]{0:T(1024)}, u32[]{:S(2)}) copy-start(s32[2048]{0:T(1024)} %param.8) | copy-start | bytes 24580
  4.4 42.0 %copy-start.1 = (bf16[2048,128]{1,0:T(8,128)(2,1)S(1)}, bf16[2048,128]{1,0:T(8,128)(2,1)}, u32[]{:S(2)}) copy-start(bf16[2048,128]{1,0:T(8,128)(2,1)} %cov_ref.3) | copy-start | bytes 1572868
  4.4 42.0 %copy-start.6 = (f32[512]{0:T(512)S(1)}, f32[512]{0:T(512)}, u32[]{:S(2)}) copy-start(f32[512]{0:T(512)} %param.10) | copy-start | bytes 6148
  46.4 0.7 %copy-start.3 = (s32[2048]{0:T(1024)S(1)}, s32[2048]{0:T(1024)}, u32[]{:S(2)}) copy-start(s32[2048]{0:T(1024)} %param.7) | copy-start | bytes 24580

commit v2 on v1

--- a/solution.py
+++ b/solution.py
@@ -41,31 +41,54 @@
     return high.astype(F32), middle.astype(F32), low.astype(F32)
 
 
+def ring(offset, size):
+    return min(offset, size - offset)
+
+
+Z_FAR = sorted(range(1, NZ), key=lambda o: -ring(o, NZ))
+XY_FAR = sorted(
+    [(dy, dx) for dy in range(4) for dx in range(4) if (dy, dx) != (0, 0)],
+    key=lambda o: -(ring(o[0], 4) + ring(o[1], 4)),
+)
+MIX_FAR = sorted(
+    [(dx, dc) for dx in range(4) for dc in range(2) if (dx, dc) != (0, 0)],
+    key=lambda o: -(ring(o[0], 4) + o[1]),
+)
+
+
 def gather_kernel(
+    samp_hbm, cov_hbm, codes_hbm, bits_hbm, noise_hbm,
+    sketch_ref, square_ref, extra_ref,
     samp_ref, cov_ref, codes_ref, bits_ref, noise_ref,
-    sketch_ref, square_ref, extra_ref,
     own, asked, picks, lhs, sent, held, rowz,
-    halves, half_in, pieces, piece_in, plane, plane_in,
-    send, recv,
+    halves, half_in, pieces, piece_in, plane_in,
+    send, recv, load,
 ):
+    loads = [
+        pltpu.make_async_copy(src, dst, load.at[i])
+        for i, (src, dst) in enumerate(
+            [
+                (samp_hbm, samp_ref), (cov_hbm, cov_ref), (codes_hbm, codes_ref),
+                (bits_hbm, bits_ref), (noise_hbm, noise_ref),
+            ]
+        )
+    ]
+    for copy in loads:
+        copy.start()
     wide = lax.axis_index("wide")
     z = lax.axis_index("narrow")
     core = lax.rem(wide, 2)
     q = wide // 2
+    x = lax.rem(q, 4)
+    y = q // 4
     member = lax.rem(wide, GROUP)
     base = wide - member
     sibling = wide + 1 - 2 * core
-
-    def mix_peer(o):
-        return lax.rem(member + o, GROUP)
-
-    def z_peer(o):
-        return lax.rem(z + o, NZ)
-
-    def xy_peer(o):
-        return lax.rem(q + o, NXY)
-
-    slots = iter(range(200))
+    mix_peers = [lax.rem(x + dx, 4) * 2 + lax.rem(core + dc, 2) for dx, dc in MIX_FAR]
+    z_peers = [lax.rem(z + o, NZ) for o in Z_FAR]
+    xy_peers = [lax.rem(y + dy, 4) * 4 + lax.rem(x + dx, 4) for dy, dx in XY_FAR]
+
+    slots = iter(range(N_COPIES))
 
     def remote(src, dst, to_wide, to_z):
         slot = next(slots)
@@ -75,34 +98,30 @@
         )
 
     barrier = pltpu.get_barrier_semaphore()
-    greeted = 0
-    for o in range(1, GROUP):
-        pl.semaphore_signal(barrier, inc=1, device_id=(base + mix_peer(o), z), device_id_type=MESH)
-        greeted += 1
-    for o in range(1, NZ):
-        pl.semaphore_signal(barrier, inc=1, device_id=(wide, z_peer(o)), device_id_type=MESH)
-        greeted += 1
-    for o in range(1, NXY):
-        pl.semaphore_signal(
-            barrier, inc=1, device_id=(2 * xy_peer(o) + core, z), device_id_type=MESH
-        )
-        greeted += 1
-
+    for peer in z_peers:
+        pl.semaphore_signal(barrier, inc=1, device_id=(wide, peer), device_id_type=MESH)
+    for peer in xy_peers:
+        pl.semaphore_signal(barrier, inc=1, device_id=(2 * peer + core, z), device_id_type=MESH)
+    for peer in mix_peers:
+        pl.semaphore_signal(barrier, inc=1, device_id=(base + peer, z), device_id_type=MESH)
+
+    loads[0].wait()
     for k in range(8):
         own[k : k + 1, :] = jnp.full((1, LANES), samp_ref[k % SAMP], jnp.int32)
     asked[member] = own[...]
-    pl.semaphore_wait(barrier, greeted)
-
-    ask = [remote(own, asked.at[member], base + mix_peer(o), z) for o in range(1, GROUP)]
+    pl.semaphore_wait(barrier, len(Z_FAR) + len(XY_FAR) + len(MIX_FAR))
+
+    ask = [remote(own, asked.at[member], base + peer, z) for peer in mix_peers]
     for copy in ask:
         copy.start()
 
+    for copy in loads[1:]:
+        copy.wait()
     codes = codes_ref[...]
     flip = cov_ref[...].astype(F32).T
+    masks = [(codes == level).astype(F32) for level in range(LEVELS)]
     for level in range(LEVELS):
-        mask = (codes == level).astype(F32)
-        lhs[level * COV : (level + 1) * COV, :] = (flip * mask).astype(BF16)
-    masks = [(codes == level).astype(F32) for level in range(LEVELS)]
+        lhs[level * COV : (level + 1) * COV, :] = (flip * masks[level]).astype(BF16)
     parts = split3(noise_ref[...])
     shadow_rows = [part * mask for part in parts for mask in masks]
     shadow_rows = jnp.concatenate(shadow_rows + [jnp.zeros((4, ROWS), F32)], axis=0)
@@ -111,7 +130,6 @@
     shadow = shadow[0:4] + shadow[4:8] + shadow[8:12]
     sub = iota((COV, COV), 0)
     lane = iota((COV, COV), 1)
-    squares = []
     diagonals = []
     for pair in range(2):
         even = normal[2 * pair * COV : (2 * pair + 1) * COV]
@@ -151,10 +169,7 @@
     for i in range(GROUP):
         sent[i] = local[i * 8 : i * 8 + SAMP].astype(BF16)
     held[member] = sent[member]
-    rows = [
-        remote(sent.at[mix_peer(o)], held.at[member], base + mix_peer(o), z)
-        for o in range(1, GROUP)
-    ]
+    rows = [remote(sent.at[peer], held.at[member], base + peer, z) for peer in mix_peers]
     for copy in rows:
         copy.start()
 
@@ -163,9 +178,9 @@
     for i in range(NZ):
         pieces[i] = jnp.concatenate([mine[i * 16 : (i + 1) * 16], mine[COV:]], axis=0)
     piece_in[z] = pieces[z]
-    a_z = [
-        remote(pieces.at[z_peer(o)], piece_in.at[z], wide, z_peer(o)) for o in range(1, NZ)
-    ]
+    a_z = [remote(pieces.at[peer], piece_in.at[z], wide, peer) for peer in z_peers]
+    for copy in a_z:
+        copy.start()
 
     for copy in rows:
         copy.wait_recv()
@@ -177,24 +192,9 @@
             for i in range(0, len(level_rows), 2)
         ]
     rowz[z] = level_rows[0].astype(BF16)
-    s_z = [remote(rowz.at[z], rowz.at[z], wide, z_peer(o)) for o in range(1, NZ)]
+    s_z = [remote(rowz.at[z], rowz.at[z], wide, peer) for peer in z_peers]
     for copy in s_z:
         copy.start()
-    for copy in a_z:
-        copy.start()
-
-    for copy in s_z:
-        copy.wait_recv()
-    stack = jnp.concatenate([rowz[i].astype(F32) for i in range(NZ)], axis=0)
-    sketch_ref[core, q] = stack.astype(BF16)
-    s_xy = [
-        remote(sketch_ref.at[core, q], sketch_ref.at[core, q], 2 * xy_peer(o) + core, z)
-        for o in range(1, NXY)
-    ]
-    for copy in s_xy:
-        copy.start()
-    s_core = [remote(sketch_ref.at[core, q], sketch_ref.at[core, q], sibling, z)]
-    s_core[0].start()
 
     for copy in a_z:
         copy.wait_recv()
@@ -202,18 +202,20 @@
     for i in range(1, NZ):
         total = total + piece_in[i]
     plane_in[q] = total
-    a_xy = [
-        remote(plane_in.at[q], plane_in.at[q], 2 * xy_peer(o) + core, z) for o in range(1, NXY)
-    ]
+    a_xy = [remote(plane_in.at[q], plane_in.at[q], 2 * peer + core, z) for peer in xy_peers]
     for copy in a_xy:
         copy.start()
 
-    for o in range(1, NXY):
-        s_xy[o - 1].wait_recv()
-        from_q = lax.rem(q - o + NXY, NXY)
-        copy = remote(sketch_ref.at[core, from_q], sketch_ref.at[core, from_q], sibling, z)
-        copy.start()
-        s_core.append(copy)
+    for copy in s_z:
+        copy.wait_recv()
+    stack = jnp.concatenate([rowz[i].astype(F32) for i in range(NZ)], axis=0)
+    block = sketch_ref.at[core, q]
+    block[...] = stack.astype(BF16)
+    s_xy = [remote(block, block, 2 * peer + core, z) for peer in xy_peers]
+    for copy in s_xy:
+        copy.start()
+    s_core = [remote(block, block, sibling, z)]
+    s_core[0].start()
 
     for copy in a_xy:
         copy.wait_recv()
@@ -222,16 +224,29 @@
         total = total + plane_in[i]
     extra_ref[...] = total[16:]
     square_ref[core, z] = total[:16]
-    a_out = [
-        remote(square_ref.at[core, z], square_ref.at[core, z], wide, z_peer(o))
-        for o in range(1, NZ)
-    ]
+    mine = square_ref.at[core, z]
+    a_out = [remote(mine, mine, wide, peer) for peer in z_peers]
     for copy in a_out:
         copy.start()
+
+    def onward(index):
+        dy, dx = XY_FAR[index]
+        s_xy[index].wait_recv()
+        from_q = lax.rem(y - dy + 4, 4) * 4 + lax.rem(x - dx + 4, 4)
+        passed = sketch_ref.at[core, from_q]
+        copy = remote(passed, passed, sibling, z)
+        copy.start()
+        s_core.append(copy)
+
+    nearest = list(range(len(XY_FAR)))[::-1]
+    for index in nearest[:10]:
+        onward(index)
     for copy in a_out:
         copy.wait_recv()
     a_last = remote(square_ref.at[core], square_ref.at[core], sibling, z)
     a_last.start()
+    for index in nearest[10:]:
+        onward(index)
     a_last.wait_recv()
     for copy in s_core:
         copy.wait_recv()
@@ -244,7 +259,7 @@
 
 def gather(samples, covariates, codes, bits, noise):
     vmem = pl.BlockSpec(memory_space=pltpu.VMEM)
-    smem = pl.BlockSpec(memory_space=pltpu.SMEM)
+    hbm = pl.BlockSpec(memory_space=pltpu.HBM)
     return pl.pallas_call(
         gather_kernel,
         out_shape=(
@@ -252,9 +267,14 @@
             jax.ShapeDtypeStruct((2, NZ, 16, COV), F32),
             jax.ShapeDtypeStruct((EXTRA, COV), F32),
         ),
-        in_specs=[smem, vmem, vmem, vmem, vmem],
+        in_specs=[hbm] * 5,
         out_specs=(vmem, vmem, vmem),
         scratch_shapes=[
+            pltpu.SMEM((SAMP,), jnp.int32),
+            pltpu.VMEM((ROWS, COV), BF16),
+            pltpu.VMEM((1, ROWS), jnp.int32),
+            pltpu.VMEM((1, ROWS), jnp.int32),
+            pltpu.VMEM((1, ROWS), F32),
             pltpu.VMEM((8, LANES), jnp.int32),
             pltpu.VMEM((GROUP, 8, LANES), jnp.int32),
             pltpu.VMEM((LEVELS * 64, ROWS), BF16),
@@ -266,10 +286,10 @@
             pltpu.VMEM((COV + EXTRA, COV), F32),
             pltpu.VMEM((NZ, 16 + EXTRA, COV), F32),
             pltpu.VMEM((NZ, 16 + EXTRA, COV), F32),
-            pltpu.VMEM((16 + EXTRA, COV), F32),
             pltpu.VMEM((NXY, 16 + EXTRA, COV), F32),
             pltpu.SemaphoreType.DMA((N_COPIES,)),
             pltpu.SemaphoreType.DMA((N_COPIES,)),
+            pltpu.SemaphoreType.DMA((5,)),
         ],
         compiler_params=pltpu.CompilerParams(
             collective_id=0, has_side_effects=True, vmem_limit_bytes=40 << 20
@@ -320,9 +340,22 @@
 
 
 def solve_kernel(
-    sketch_ref, square_ref, extra_ref, effects_ref, cov_ref, codes_ref, noise_ref,
-    coef_ref, resid_ref, factor_ref, gram, inverse,
+    sketch_ref, square_ref, extra_ref, effects_hbm, cov_hbm, codes_hbm, noise_hbm,
+    coef_ref, resid_ref, factor_hbm, gram, inverse,
+    factor_ref, effects_ref, cov_ref, codes_ref, noise_ref, load, store,
 ):
+    loads = [
+        pltpu.make_async_copy(src, dst, load.at[i])
+        for i, (src, dst) in enumerate(
+            [
+                (effects_hbm, effects_ref), (cov_hbm, cov_ref), (codes_hbm, codes_ref),
+                (noise_hbm, noise_ref),
+            ]
+        )
+    ]
+    for copy in loads:
+        copy.start()
+    stores = []
     n = LEVELS
     sub = iota((COV, COV), 0)
     lane = iota((COV, COV), 1)
@@ -342,6 +375,9 @@
         factor_ref[blk(k), blk(k)] = jnp.where(lane >= sub, product[:, blk(k)], 0.0) * scale
         if k + 1 < n:
             factor_ref[blk(k), (k + 1) * COV :] = product[:, (k + 1) * COV :] * scale
+        part = pltpu.make_async_copy(factor_ref.at[blk(k)], factor_hbm.at[blk(k)], store.at[k])
+        part.start()
+        stores.append(part)
         for i in range(k + 1, n):
             back = product[:, blk(i)].T
             change = jnp.dot(back, product[:, i * COV :], precision=HIGH, preferred_element_type=F32)
@@ -392,6 +428,8 @@
             acc = acc + a * b
         return jnp.sum(acc, axis=axis, keepdims=True)
 
+    for copy in loads:
+        copy.wait()
     effects = [effects_ref[:, blk(level)] for level in range(n)]
     gradient = [
         image + extra_ref[level : level + 1, :] for level, image in enumerate(apply_normal(effects))
@@ -426,10 +464,13 @@
         value = values[level : level + 1] + values[4 + level : 5 + level] + values[8 + level : 9 + level]
         resid = resid + jnp.where(codes == level, value, 0.0)
     resid_ref[...] = resid
+    for copy in stores:
+        copy.wait()
 
 
 def solve(sketch, square, extra, effects, covariates, codes, noise):
     vmem = pl.BlockSpec(memory_space=pltpu.VMEM)
+    hbm = pl.BlockSpec(memory_space=pltpu.HBM)
     return pl.pallas_call(
         solve_kernel,
         out_shape=(
@@ -437,11 +478,18 @@
             jax.ShapeDtypeStruct((1, ROWS), F32),
             jax.ShapeDtypeStruct((COLS, COLS), F32),
         ),
-        in_specs=[vmem] * 7,
-        out_specs=(vmem,) * 3,
+        in_specs=[vmem] * 3 + [hbm] * 4,
+        out_specs=(vmem, vmem, hbm),
         scratch_shapes=[
             pltpu.VMEM((LEVELS, COV, COLS), F32),
             pltpu.VMEM((LEVELS, COV, COLS), F32),
+            pltpu.VMEM((COLS, COLS), F32),
+            pltpu.VMEM((1, COLS), F32),
+            pltpu.VMEM((ROWS, COV), BF16),
+            pltpu.VMEM((1, ROWS), jnp.int32),
+            pltpu.VMEM((1, ROWS), F32),
+            pltpu.SemaphoreType.DMA((4,)),
+            pltpu.SemaphoreType.DMA((LEVELS,)),
         ],
         compiler_params=pltpu.CompilerParams(vmem_limit_bytes=40 << 20),
         name="solve",
@@ -449,14 +497,18 @@
 
 
 def body(covariates, level_codes, sign_bits, sample_rows, effects, noise):
-    codes = level_codes.reshape(1, ROWS)
-    noise = noise.reshape(1, ROWS)
+    def fixed(value):
+        return pltpu.with_memory_space_constraint(value, pltpu.HBM)
+
+    covariates = fixed(covariates)
+    codes = fixed(level_codes.reshape(1, ROWS))
+    noise = fixed(noise.reshape(1, ROWS))
     sketch, square, extra = gather(
-        sample_rows, covariates, codes, sign_bits.reshape(1, ROWS), noise
+        fixed(sample_rows), covariates, codes, fixed(sign_bits.reshape(1, ROWS)), noise
     )
     coef, resid, factor = solve(
         sketch.reshape(SKETCH, COLS), square.reshape(2, COV, COV), extra,
-        effects.reshape(1, COLS), covariates, codes, noise,
+        fixed(effects.reshape(1, COLS)), covariates, codes, noise,
     )
     return coef.reshape(COLS), resid.reshape(ROWS), factor
 

time: 69.7 us -> 57.7 us (0.83)
  Pallas kernels: 64.2 us -> 56.7 us
  local copies, waits for them, and re-layouts: 4.46 us -> 0 us
    pallas_call x1, Pallas kernels: 42 us -> 33.9 us  [gather(): pl.pallas_call(gather_kernel, out_shape=(jax.ShapeDtypeStruct((2, NXY, 32...]
    unnamed x16 -> x0, local copies, waits for them, and re-layouts: 4.46 us -> none
where the time goes in v2:
time: 57.7 us; the launch traced here: 57.5 us
  Pallas kernels  56.7 us (98%)
  between operations  0.8 us (1%)
    pallas_call x1, Pallas kernels, gather(): pl.pallas_call(gather_kernel, out_shape=(jax.ShapeDtypeStruct((2, NXY, 32...  33.9 us
    pallas_call x1, Pallas kernels, solve(): pl.pallas_call(solve_kernel, out_shape=(jax.ShapeDtypeStruct((1, COLS), F...  22.8 us

profile of v2, /device:TPU:1, one launch (start us, length us, event | category | flops | bytes accessed | tf_op | source)
XLA Modules:
  0.0 57.5 jit_solution(12727466529950623996)
XLA Ops:
  0.6 33.9 %gather_sketch.1 = (bf16[2,16,32,512]{3,2,1,0:T(8,128)(2,1)S(1)}, f32[2,8,16,128]{3,2,1,0:T(8,128)S(1)}, f32[8,128]{1,0:T(8,128)S(1)}) custom-call(s32[4]{0:T(128)} %samp_hbm.1, bf16[2048,128]{1,0:T(8,128)(2,1)} %cov_hbm.3, s32[1,2048]{1,0:T(1,128)} %bitcast.10, s32[1,2048]{1,0:T(1,128)} %bitcast.14, f32[1,2048]{1,0:T(1,128)} %bitcast.12), custom_call_target="tpu_custom_call" | custom-call | tf_op jit(solution)/shard_map/gather_sketch/pallas_call | solution.py:263
  34.5 22.8 %solve.1 = (f32[1,512]{1,0:T(1,128)}, f32[1,2048]{1,0:T(1,128)}, f32[512,512]{1,0:T(8,128)}) custom-call(bf16[1024,512]{1,0:T(8,128)(2,1)S(1)} %bitcast.8, f32[2,128,128]{2,1,0:T(8,128)S(1)} %bitcast.9, f32[8,128]{1,0:T(8,128)S(1)} %get-tuple-element.11.extra_ref, f32[1,512]{1,0:T(1,128)} %bitcast.15, bf16[2048,128]{1,0:T(8,128)(2,1)} %cov_hbm.3, ...), custom_call_target="tpu_custom_call" | custom-call | tf_op jit(solution)/shard_map/solve/pallas_call | solution.py:474

commit v3 on v2

--- a/solution.py
+++ b/solution.py
@@ -18,7 +18,8 @@
 ITERS = 4
 GROUP = 8
 NZ = 8
-NXY = 16
+NX = 4
+NY = 4
 EXTRA = 8
 LANES = 128
 
@@ -46,10 +47,7 @@
 
 
 Z_FAR = sorted(range(1, NZ), key=lambda o: -ring(o, NZ))
-XY_FAR = sorted(
-    [(dy, dx) for dy in range(4) for dx in range(4) if (dy, dx) != (0, 0)],
-    key=lambda o: -(ring(o[0], 4) + ring(o[1], 4)),
-)
+FOUR_FAR = (2, 1, 3)
 MIX_FAR = sorted(
     [(dx, dc) for dx in range(4) for dc in range(2) if (dx, dc) != (0, 0)],
     key=lambda o: -(ring(o[0], 4) + o[1]),
@@ -61,7 +59,7 @@
     sketch_ref, square_ref, extra_ref,
     samp_ref, cov_ref, codes_ref, bits_ref, noise_ref,
     own, asked, picks, lhs, sent, held, rowz,
-    halves, half_in, pieces, piece_in, plane_in,
+    halves, half_in, pieces, piece_in, row_in, col_in,
     send, recv, load,
 ):
     loads = [
@@ -86,7 +84,8 @@
     sibling = wide + 1 - 2 * core
     mix_peers = [lax.rem(x + dx, 4) * 2 + lax.rem(core + dc, 2) for dx, dc in MIX_FAR]
     z_peers = [lax.rem(z + o, NZ) for o in Z_FAR]
-    xy_peers = [lax.rem(y + dy, 4) * 4 + lax.rem(x + dx, 4) for dy, dx in XY_FAR]
+    x_peers = [(y * 4 + lax.rem(x + o, 4)) * 2 + core for o in FOUR_FAR]
+    y_peers = [(lax.rem(y + o, 4) * 4 + x) * 2 + core for o in FOUR_FAR]
 
     slots = iter(range(N_COPIES))
 
@@ -100,8 +99,8 @@
     barrier = pltpu.get_barrier_semaphore()
     for peer in z_peers:
         pl.semaphore_signal(barrier, inc=1, device_id=(wide, peer), device_id_type=MESH)
-    for peer in xy_peers:
-        pl.semaphore_signal(barrier, inc=1, device_id=(2 * peer + core, z), device_id_type=MESH)
+    for peer in y_peers:
+        pl.semaphore_signal(barrier, inc=1, device_id=(peer, z), device_id_type=MESH)
     for peer in mix_peers:
         pl.semaphore_signal(barrier, inc=1, device_id=(base + peer, z), device_id_type=MESH)
 
@@ -109,7 +108,7 @@
     for k in range(8):
         own[k : k + 1, :] = jnp.full((1, LANES), samp_ref[k % SAMP], jnp.int32)
     asked[member] = own[...]
-    pl.semaphore_wait(barrier, len(Z_FAR) + len(XY_FAR) + len(MIX_FAR))
+    pl.semaphore_wait(barrier, len(Z_FAR) + len(FOUR_FAR) + len(MIX_FAR))
 
     ask = [remote(own, asked.at[member], base + peer, z) for peer in mix_peers]
     for copy in ask:
@@ -152,6 +151,7 @@
     low = common ^ (common >> 1)
     top = (want >> 7) & 1
     block = want >> 8
+    upper_half = (iota(shape, 0) // SAMP) & 1
     for chunk in range(ROWS // LANES):
         span = slice(chunk * LANES, (chunk + 1) * LANES)
         parity = low ^ bits_ref[:, span]
@@ -160,14 +160,14 @@
         sign = (1 - 2 * (parity & 1)).astype(F32)
         sign = jnp.where(block == chunk // 2, sign, 0.0)
         here = codes_ref[:, span]
-        for level in range(LEVELS):
-            value = sign * (here == level).astype(F32)
-            picks[level * 64 : (level + 1) * 64, span] = value.astype(BF16)
+        for pair in range(2):
+            value = jnp.where(here == 2 * pair + upper_half, sign, 0.0)
+            picks[pair * 64 : (pair + 1) * 64, span] = value.astype(BF16)
     local = jnp.dot(picks[...], cov_ref[...], preferred_element_type=F32)
     local = local * (1.0 / math.sqrt(HB))
-    local = jnp.concatenate([local[level * 64 : (level + 1) * 64] for level in range(LEVELS)], axis=1)
     for i in range(GROUP):
-        sent[i] = local[i * 8 : i * 8 + SAMP].astype(BF16)
+        spots = [pair * 64 + i * 8 + SAMP * half for pair in range(2) for half in range(2)]
+        sent[i] = jnp.concatenate([local[at : at + SAMP] for at in spots], axis=1).astype(BF16)
     held[member] = sent[member]
     rows = [remote(sent.at[peer], held.at[member], base + peer, z) for peer in mix_peers]
     for copy in rows:
@@ -201,27 +201,52 @@
     total = piece_in[0]
     for i in range(1, NZ):
         total = total + piece_in[i]
-    plane_in[q] = total
-    a_xy = [remote(plane_in.at[q], plane_in.at[q], 2 * peer + core, z) for peer in xy_peers]
-    for copy in a_xy:
+    row_in[x] = total
+    a_x = [remote(row_in.at[x], row_in.at[x], peer, z) for peer in x_peers]
+    for copy in a_x:
         copy.start()
 
     for copy in s_z:
         copy.wait_recv()
-    stack = jnp.concatenate([rowz[i].astype(F32) for i in range(NZ)], axis=0)
-    block = sketch_ref.at[core, q]
-    block[...] = stack.astype(BF16)
-    s_xy = [remote(block, block, 2 * peer + core, z) for peer in xy_peers]
-    for copy in s_xy:
-        copy.start()
-    s_core = [remote(block, block, sibling, z)]
-    s_core[0].start()
-
-    for copy in a_xy:
-        copy.wait_recv()
-    total = plane_in[0]
-    for i in range(1, NXY):
-        total = total + plane_in[i]
+    stack = jnp.concatenate([rowz[i].astype(F32) for i in range(NZ)], axis=0).astype(BF16)
+    sketch_ref[0, core, y, x] = stack[:16]
+    sketch_ref[1, core, x, y] = stack[16:]
+    first = sketch_ref.at[0, core, y, x]
+    second = sketch_ref.at[1, core, x, y]
+    s_first = [remote(first, first, peer, z) for peer in x_peers]
+    s_second = [remote(second, second, peer, z) for peer in y_peers]
+    for one, two in zip(s_first, s_second):
+        one.start()
+        two.start()
+
+    for copy in a_x:
+        copy.wait_recv()
+    total = row_in[0]
+    for i in range(1, NX):
+        total = total + row_in[i]
+    col_in[y] = total
+    a_y = [remote(col_in.at[y], col_in.at[y], peer, z) for peer in y_peers]
+    for copy in a_y:
+        copy.start()
+
+    for copy in s_first + s_second:
+        copy.wait_recv()
+    line = sketch_ref.at[0, core, y]
+    other = sketch_ref.at[1, core, x]
+    s_line = [remote(line, line, peer, z) for peer in y_peers]
+    s_other = [remote(other, other, peer, z) for peer in x_peers]
+    for one, two in zip(s_line, s_other):
+        one.start()
+        two.start()
+    s_core = [remote(line, line, sibling, z), remote(other, other, sibling, z)]
+    for copy in s_core:
+        copy.start()
+
+    for copy in a_y:
+        copy.wait_recv()
+    total = col_in[0]
+    for i in range(1, NY):
+        total = total + col_in[i]
     extra_ref[...] = total[16:]
     square_ref[core, z] = total[:16]
     mine = square_ref.at[core, z]
@@ -230,31 +255,33 @@
         copy.start()
 
     def onward(index):
-        dy, dx = XY_FAR[index]
-        s_xy[index].wait_recv()
-        from_q = lax.rem(y - dy + 4, 4) * 4 + lax.rem(x - dx + 4, 4)
-        passed = sketch_ref.at[core, from_q]
+        s_line[index].wait_recv()
+        passed = sketch_ref.at[0, core, lax.rem(y - FOUR_FAR[index] + 4, 4)]
         copy = remote(passed, passed, sibling, z)
         copy.start()
         s_core.append(copy)
-
-    nearest = list(range(len(XY_FAR)))[::-1]
-    for index in nearest[:10]:
-        onward(index)
+        s_other[index].wait_recv()
+        passed = sketch_ref.at[1, core, lax.rem(x - FOUR_FAR[index] + 4, 4)]
+        copy = remote(passed, passed, sibling, z)
+        copy.start()
+        s_core.append(copy)
+
+    onward(1)
+    onward(2)
     for copy in a_out:
         copy.wait_recv()
     a_last = remote(square_ref.at[core], square_ref.at[core], sibling, z)
     a_last.start()
-    for index in nearest[10:]:
-        onward(index)
+    onward(0)
     a_last.wait_recv()
     for copy in s_core:
         copy.wait_recv()
-    for copy in ask + [a_core] + rows + a_z + s_z + s_xy + a_xy + s_core + a_out + [a_last]:
+    sums = [a_core] + a_z + a_x + a_y + a_out + [a_last]
+    for copy in ask + rows + s_z + s_first + s_second + s_line + s_other + s_core + sums:
         copy.wait_send()
 
 
-N_COPIES = 3 * 7 + 1 + 7 + 1 + 15 + 15 + 15 + 7 + 1
+N_COPIES = 7 + 1 + 7 + 7 + 7 + 3 + 6 + 3 + 6 + 8 + 7 + 1
 
 
 def gather(samples, covariates, codes, bits, noise):
@@ -263,7 +290,7 @@
     return pl.pallas_call(
         gather_kernel,
         out_shape=(
-            jax.ShapeDtypeStruct((2, NXY, 32, COLS), BF16),
+            jax.ShapeDtypeStruct((2, 2, 4, 4, 16, COLS), BF16),
             jax.ShapeDtypeStruct((2, NZ, 16, COV), F32),
             jax.ShapeDtypeStruct((EXTRA, COV), F32),
         ),
@@ -277,7 +304,7 @@
             pltpu.VMEM((1, ROWS), F32),
             pltpu.VMEM((8, LANES), jnp.int32),
             pltpu.VMEM((GROUP, 8, LANES), jnp.int32),
-            pltpu.VMEM((LEVELS * 64, ROWS), BF16),
+            pltpu.VMEM((2 * 64, ROWS), BF16),
             pltpu.VMEM((COLS, ROWS), BF16),
             pltpu.VMEM((GROUP, SAMP, COLS), BF16),
             pltpu.VMEM((GROUP, SAMP, COLS), BF16),
@@ -286,7 +313,8 @@
             pltpu.VMEM((COV + EXTRA, COV), F32),
             pltpu.VMEM((NZ, 16 + EXTRA, COV), F32),
             pltpu.VMEM((NZ, 16 + EXTRA, COV), F32),
-            pltpu.VMEM((NXY, 16 + EXTRA, COV), F32),
+            pltpu.VMEM((NX, 16 + EXTRA, COV), F32),
+            pltpu.VMEM((NY, 16 + EXTRA, COV), F32),
             pltpu.SemaphoreType.DMA((N_COPIES,)),
             pltpu.SemaphoreType.DMA((N_COPIES,)),
             pltpu.SemaphoreType.DMA((5,)),
@@ -302,34 +330,62 @@
     return jnp.broadcast_to(value[index : index + 1, :], value.shape)
 
 
-def invert_factor(matrix):
+def column(value, index):
+    return jnp.broadcast_to(value[:, index : index + 1], value.shape)
+
+
+def invert_factor(matrix, ahead=2):
     count = COV // 8
     rows = [matrix[8 * t : 8 * t + 8, :] for t in range(count)]
     sub = iota((8, COV), 0)
     lane = iota((8, COV), 1)
     for p in range(count):
         first = 8 * p
-        own = [
-            [jnp.broadcast_to(rows[t][:, first + i : first + i + 1], (8, COV)) for t in range(p, count)]
-            for i in range(8)
-        ]
         panel = (lane >= first) & (lane < first + 8)
-        for t in range(p + 1, count):
-            rows[t] = jnp.where(panel, 0.0, rows[t])
+        near = range(p, min(p + 1 + ahead, count))
+        own = {t: [column(rows[t], first + i) for i in range(8)] for t in near}
+        left = [[spread(own[p][c], a) for c in range(a + 1)] for a in range(8)]
         rows[p] = jnp.where(panel, jnp.where(lane == first + sub, 1.0, 0.0), rows[p])
+        start = [spread(rows[p], i) for i in range(8)]
+        root = []
+        low = [[None] * 8 for _ in range(8)]
         for i in range(8):
-            root = lax.rsqrt(spread(own[i][0], i))
-            row = spread(rows[p], i) * root
-            upper = {k: spread(own[k][0], i) * root for k in range(i + 1, 8)}
-            for t in range(p, count):
-                scale = own[i][t - p] * root
-                if t == p:
-                    scale = jnp.where(sub > i, scale, 0.0)
-                    rows[t] = jnp.where(sub == i, row, rows[t] - scale * row)
-                else:
-                    rows[t] = rows[t] - scale * row
-                for k in range(i + 1, 8):
-                    own[k][t - p] = own[k][t - p] - scale * upper[k]
+            root.append(lax.rsqrt(left[i][i]))
+            for a in range(i + 1, 8):
+                low[a][i] = left[a][i] * root[i]
+            for a in range(i + 1, 8):
+                for c in range(i + 1, a + 1):
+                    left[a][c] = left[a][c] - low[a][i] * low[c][i]
+        row = []
+        for i in range(8):
+            value = start[i]
+            for k in range(i):
+                value = value - low[i][k] * row[k]
+            row.append(value * root[i])
+        value = row[7]
+        for i in range(7):
+            value = jnp.where(sub == i, row[i], value)
+        rows[p] = value
+        far = range(p + 1 + ahead, count)
+        if len(far):
+            high, middle, small = split3(value)
+            one = jnp.concatenate([high, high, high, middle, middle, small], axis=0).astype(BF16)
+            two = jnp.concatenate([high, middle, small, high, middle, high], axis=0).astype(BF16)
+            change = lax.dot_general(
+                one, two, (((0,), (0,)), ((), ())), preferred_element_type=F32
+            )
+        for t in near[1:]:
+            value = jnp.where(panel, 0.0, rows[t])
+            scales = []
+            for i in range(8):
+                scale = own[t][i]
+                for k in range(i):
+                    scale = scale - scales[k] * low[i][k]
+                scales.append(scale * root[i])
+                value = value - scales[i] * row[i]
+            rows[t] = value
+        for t in far:
+            rows[t] = jnp.where(panel, 0.0, rows[t]) - change[8 * t : 8 * t + 8, :]
     for p in range(count):
         rows[p] = jnp.where(lane <= 8 * p + sub, rows[p], 0.0)
     return jnp.concatenate(rows, axis=0)

time: 57.7 us -> 55.5 us (0.962)
  Pallas kernels: 56.7 us -> 54.6 us
    pallas_call x1, Pallas kernels: 22.8 us -> 21 us  [solve(): pl.pallas_call(solve_kernel, out_shape=(jax.ShapeDtypeStruct((1, COLS), F...]
where the time goes in v3:
time: 55.5 us; the launch traced here: 55.4 us
  Pallas kernels  54.6 us (98%)
  between operations  0.8 us (1%)
    pallas_call x1, Pallas kernels, gather(): pl.pallas_call(gather_kernel, out_shape=(jax.ShapeDtypeStruct((2, 2, 4, 4...  33.6 us
    pallas_call x1, Pallas kernels, solve(): pl.pallas_call(solve_kernel, out_shape=(jax.ShapeDtypeStruct((1, COLS), F...  21 us

profile of v3, /device:TPU:1, one launch (start us, length us, event | category | flops | bytes accessed | tf_op | source)
XLA Modules:
  0.0 55.4 jit_solution(3283731378684234249)
XLA Ops:
  0.6 33.6 %gather_sketch.1 = (bf16[2,2,4,4,16,512]{5,4,3,2,1,0:T(8,128)(2,1)S(1)}, f32[2,8,16,128]{3,2,1,0:T(8,128)S(1)}, f32[8,128]{1,0:T(8,128)S(1)}) custom-call(s32[4]{0:T(128)} %samp_hbm.1, bf16[2048,128]{1,0:T(8,128)(2,1)} %cov_hbm.3, s32[1,2048]{1,0:T(1,128)} %bitcast.10, s32[1,2048]{1,0:T(1,128)} %bitcast.14, f32[1,2048]{1,0:T(1,128)} %bitcast.12), custom_call_target="tpu_custom_call" | custom-call | tf_op jit(solution)/shard_map/gather_sketch/pallas_call | solution.py:290
  34.3 21.0 %solve.1 = (f32[1,512]{1,0:T(1,128)}, f32[1,2048]{1,0:T(1,128)}, f32[512,512]{1,0:T(8,128)}) custom-call(bf16[1024,512]{1,0:T(8,128)(2,1)S(1)} %bitcast.8, f32[2,128,128]{2,1,0:T(8,128)S(1)} %bitcast.9, f32[8,128]{1,0:T(8,128)S(1)} %get-tuple-element.11.extra_ref, f32[1,512]{1,0:T(1,128)} %bitcast.15, bf16[2048,128]{1,0:T(8,128)(2,1)} %cov_hbm.3, ...), custom_call_target="tpu_custom_call" | custom-call | tf_op jit(solution)/shard_map/solve/pallas_call | solution.py:530

commit v4 on v3

--- a/solution.py
+++ b/solution.py
@@ -326,68 +326,107 @@
     )(samples, covariates, codes, bits, noise)
 
 
-def spread(value, index):
-    return jnp.broadcast_to(value[index : index + 1, :], value.shape)
-
-
 def column(value, index):
     return jnp.broadcast_to(value[:, index : index + 1], value.shape)
 
 
-def invert_factor(matrix, ahead=2):
-    count = COV // 8
-    rows = [matrix[8 * t : 8 * t + 8, :] for t in range(count)]
-    sub = iota((8, COV), 0)
-    lane = iota((8, COV), 1)
+def six(value, order, axis):
+    parts = split3(value)
+    return jnp.concatenate([parts[i] for i in order], axis=axis).astype(BF16)
+
+
+def product6(left, right, turned=False):
+    axis = 0 if turned else 1
+    return lax.dot_general(
+        six(left, (0, 0, 0, 1, 1, 2), axis), six(right, (0, 1, 2, 0, 1, 0), 0),
+        (((axis,), (0,)), ((), ())), preferred_element_type=F32,
+    )
+
+
+AHEAD = 4
+PANEL = 8
+SLOTS = 2 * PANEL + 1
+
+
+def invert_factor(matrix, slots):
+    count = COV // PANEL
+    shape = (PANEL, COV)
+    rows = [matrix[PANEL * t : PANEL * (t + 1), :] for t in range(count)]
+    sub = iota(shape, 0)
+    lane = iota(shape, 1)
+
+    def columns(t, first):
+        return [column(rows[t], first + i) for i in range(PANEL)]
+
+    def spread(slot, index):
+        return slots[slot, pl.ds(index, PANEL, stride=0), :]
+
+    pivot = columns(0, 0)
     for p in range(count):
-        first = 8 * p
-        panel = (lane >= first) & (lane < first + 8)
-        near = range(p, min(p + 1 + ahead, count))
-        own = {t: [column(rows[t], first + i) for i in range(8)] for t in near}
-        left = [[spread(own[p][c], a) for c in range(a + 1)] for a in range(8)]
+        base = (p % 2) * SLOTS
+        first = PANEL * p
+        panel = (lane >= first) & (lane < first + PANEL)
+        near = range(p + 1, min(p + 1 + AHEAD, count))
+        far = range(min(p + 1 + AHEAD, count), count)
+        own = {t: columns(t, first) for t in near}
+        after = columns(p + 1, first + PANEL) if p + 1 < count else None
+        for c in range(PANEL):
+            slots[base + c] = pivot[c]
+        left = [[spread(base + c, a) for c in range(a + 1)] for a in range(PANEL)]
         rows[p] = jnp.where(panel, jnp.where(lane == first + sub, 1.0, 0.0), rows[p])
-        start = [spread(rows[p], i) for i in range(8)]
+        slots[base + PANEL] = rows[p]
+        start = [spread(base + PANEL, i) for i in range(PANEL)]
         root = []
-        low = [[None] * 8 for _ in range(8)]
-        for i in range(8):
+        low = [[None] * PANEL for _ in range(PANEL)]
+        for i in range(PANEL):
             root.append(lax.rsqrt(left[i][i]))
-            for a in range(i + 1, 8):
+            for a in range(i + 1, PANEL):
                 low[a][i] = left[a][i] * root[i]
-            for a in range(i + 1, 8):
+            for a in range(i + 1, PANEL):
                 for c in range(i + 1, a + 1):
                     left[a][c] = left[a][c] - low[a][i] * low[c][i]
+
+        def multipliers(t):
+            scales = []
+            for i in range(PANEL):
+                scale = own[t][i]
+                for k in range(i):
+                    scale = scale - scales[k] * low[i][k]
+                scales.append(scale * root[i])
+            return scales
+
+        scales = {}
+        if after:
+            scales[p + 1] = multipliers(p + 1)
+            for i, scale in enumerate(scales[p + 1]):
+                slot = base + PANEL + 1 + i
+                slots[slot] = scale
+                for c in range(PANEL):
+                    after[c] = after[c] - scale * spread(slot, c)
+            pivot = after
         row = []
-        for i in range(8):
+        for i in range(PANEL):
             value = start[i]
             for k in range(i):
                 value = value - low[i][k] * row[k]
             row.append(value * root[i])
-        value = row[7]
-        for i in range(7):
+        value = row[PANEL - 1]
+        for i in range(PANEL - 1):
             value = jnp.where(sub == i, row[i], value)
         rows[p] = value
-        far = range(p + 1 + ahead, count)
         if len(far):
-            high, middle, small = split3(value)
-            one = jnp.concatenate([high, high, high, middle, middle, small], axis=0).astype(BF16)
-            two = jnp.concatenate([high, middle, small, high, middle, high], axis=0).astype(BF16)
-            change = lax.dot_general(
-                one, two, (((0,), (0,)), ((), ())), preferred_element_type=F32
-            )
-        for t in near[1:]:
+            change = product6(value, value, turned=True)
+        for t in near:
+            if t not in scales:
+                scales[t] = multipliers(t)
             value = jnp.where(panel, 0.0, rows[t])
-            scales = []
-            for i in range(8):
-                scale = own[t][i]
-                for k in range(i):
-                    scale = scale - scales[k] * low[i][k]
-                scales.append(scale * root[i])
-                value = value - scales[i] * row[i]
+            for scale, one in zip(scales[t], row):
+                value = value - scale * one
             rows[t] = value
         for t in far:
-            rows[t] = jnp.where(panel, 0.0, rows[t]) - change[8 * t : 8 * t + 8, :]
+            rows[t] = jnp.where(panel, 0.0, rows[t]) - change[PANEL * t : PANEL * (t + 1), :]
     for p in range(count):
-        rows[p] = jnp.where(lane <= 8 * p + sub, rows[p], 0.0)
+        rows[p] = jnp.where(lane <= PANEL * p + sub, rows[p], 0.0)
     return jnp.concatenate(rows, axis=0)
 
 
@@ -398,7 +437,7 @@
 def solve_kernel(
     sketch_ref, square_ref, extra_ref, effects_hbm, cov_hbm, codes_hbm, noise_hbm,
     coef_ref, resid_ref, factor_hbm, gram, inverse,
-    factor_ref, effects_ref, cov_ref, codes_ref, noise_ref, load, store,
+    factor_ref, effects_ref, cov_ref, codes_ref, noise_ref, slots, load, store,
 ):
     loads = [
         pltpu.make_async_copy(src, dst, load.at[i])
@@ -421,29 +460,40 @@
             sketch_ref[:, blk(k)], sketch_ref[:, k * COV :], (((0,), (0,)), ((), ())),
             preferred_element_type=F32,
         )
+    matrix = gram[0, :, blk(0)]
     for k in range(n):
-        corner = invert_factor(gram[k, :, blk(k)])
+        current = matrix
+        corner = invert_factor(current, slots)
         inverse[k, :, blk(k)] = corner
-        product = jnp.dot(corner, gram[k], precision=HIGH, preferred_element_type=F32)
+        head = None
+        if k + 1 < n:
+            head = product6(corner, gram[k, :, blk(k + 1)])
+            matrix = gram[k + 1, :, blk(k + 1)] - product6(head, head, turned=True)
         if k:
-            inverse[k, :, : k * COV] = product[:, : k * COV]
+            inverse[k, :, : k * COV] = product6(corner, gram[k, :, : k * COV])
             factor_ref[blk(k), : k * COV] = jnp.zeros((COV, k * COV), F32)
-        factor_ref[blk(k), blk(k)] = jnp.where(lane >= sub, product[:, blk(k)], 0.0) * scale
+        own = product6(corner, current)
+        factor_ref[blk(k), blk(k)] = jnp.where(lane >= sub, own, 0.0) * scale
+        upper = {k + 1: head}
         if k + 1 < n:
-            factor_ref[blk(k), (k + 1) * COV :] = product[:, (k + 1) * COV :] * scale
+            factor_ref[blk(k), blk(k + 1)] = head * scale
+        if k + 2 < n:
+            rest = product6(corner, gram[k, :, (k + 2) * COV :])
+            factor_ref[blk(k), (k + 2) * COV :] = rest * scale
+            for i in range(k + 2, n):
+                upper[i] = rest[:, blk(i - k - 2)]
         part = pltpu.make_async_copy(factor_ref.at[blk(k)], factor_hbm.at[blk(k)], store.at[k])
         part.start()
         stores.append(part)
         for i in range(k + 1, n):
-            back = product[:, blk(i)].T
-            change = jnp.dot(back, product[:, i * COV :], precision=HIGH, preferred_element_type=F32)
-            gram[i, :, i * COV :] = gram[i, :, i * COV :] - change
-        for i in range(k + 1, n):
-            back = product[:, blk(i)].T
-            gram[i, :, blk(k)] = -jnp.dot(back, corner, precision=HIGH, preferred_element_type=F32)
+            for j in range(i, n):
+                if j > k + 1:
+                    change = product6(upper[i], upper[j], turned=True)
+                    gram[i, :, blk(j)] = gram[i, :, blk(j)] - change
+            change = product6(upper[i], inverse[k, :, : (k + 1) * COV], turned=True)
             if k:
-                change = jnp.dot(back, product[:, : k * COV], precision=HIGH, preferred_element_type=F32)
-                gram[i, :, : k * COV] = gram[i, :, : k * COV] - change
+                gram[i, :, : k * COV] = gram[i, :, : k * COV] - change[:, : k * COV]
+            gram[i, :, blk(k)] = -change[:, blk(k)]
 
     normal = []
     for pair in range(2):
@@ -544,6 +594,7 @@
             pltpu.VMEM((ROWS, COV), BF16),
             pltpu.VMEM((1, ROWS), jnp.int32),
             pltpu.VMEM((1, ROWS), F32),
+            pltpu.VMEM((2 * SLOTS, PANEL, COV), F32),
             pltpu.SemaphoreType.DMA((4,)),
             pltpu.SemaphoreType.DMA((LEVELS,)),
         ],

time: 55.5 us -> 49.1 us (0.88)
  Pallas kernels: 54.6 us -> 48.3 us
    pallas_call x1, Pallas kernels: 21 us -> 14.7 us  [solve(): pl.pallas_call(solve_kernel, out_shape=(jax.ShapeDtypeStruct((1, COLS), F...]
where the time goes in v4:
time: 49.1 us; the launch traced here: 49 us
  Pallas kernels  48.3 us (98%)
  between operations  0.64 us (1%)
    pallas_call x1, Pallas kernels, gather(): pl.pallas_call(gather_kernel, out_shape=(jax.ShapeDtypeStruct((2, 2, 4, 4...  33.6 us
    pallas_call x1, Pallas kernels, solve(): pl.pallas_call(solve_kernel, out_shape=(jax.ShapeDtypeStruct((1, COLS), F...  14.7 us

profile of v4, /device:TPU:1, one launch (start us, length us, event | category | flops | bytes accessed | tf_op | source)
XLA Modules:
  0.0 49.0 jit_solution(17989664171013650694)
XLA Ops:
  0.6 33.6 %gather_sketch.1 = (bf16[2,2,4,4,16,512]{5,4,3,2,1,0:T(8,128)(2,1)S(1)}, f32[2,8,16,128]{3,2,1,0:T(8,128)S(1)}, f32[8,128]{1,0:T(8,128)S(1)}) custom-call(s32[4]{0:T(128)} %samp_hbm.1, bf16[2048,128]{1,0:T(8,128)(2,1)} %cov_hbm.3, s32[1,2048]{1,0:T(1,128)} %bitcast.10, s32[1,2048]{1,0:T(1,128)} %bitcast.14, f32[1,2048]{1,0:T(1,128)} %bitcast.12), custom_call_target="tpu_custom_call" | custom-call | tf_op jit(solution)/shard_map/gather_sketch/pallas_call | solution.py:290
  34.3 14.7 %solve.1 = (f32[1,512]{1,0:T(1,128)}, f32[1,2048]{1,0:T(1,128)}, f32[512,512]{1,0:T(8,128)}) custom-call(bf16[1024,512]{1,0:T(8,128)(2,1)S(1)} %bitcast.8, f32[2,128,128]{2,1,0:T(8,128)S(1)} %bitcast.9, f32[8,128]{1,0:T(8,128)S(1)} %get-tuple-element.11.extra_ref, f32[1,512]{1,0:T(1,128)} %bitcast.15, bf16[2048,128]{1,0:T(8,128)(2,1)} %cov_hbm.3, ...), custom_call_target="tpu_custom_call" | custom-call | tf_op jit(solution)/shard_map/solve/pallas_call | solution.py:580

commit v5 on v4

--- a/solution.py
+++ b/solution.py
@@ -103,16 +103,6 @@
         pl.semaphore_signal(barrier, inc=1, device_id=(peer, z), device_id_type=MESH)
     for peer in mix_peers:
         pl.semaphore_signal(barrier, inc=1, device_id=(base + peer, z), device_id_type=MESH)
-
-    loads[0].wait()
-    for k in range(8):
-        own[k : k + 1, :] = jnp.full((1, LANES), samp_ref[k % SAMP], jnp.int32)
-    asked[member] = own[...]
-    pl.semaphore_wait(barrier, len(Z_FAR) + len(FOUR_FAR) + len(MIX_FAR))
-
-    ask = [remote(own, asked.at[member], base + peer, z) for peer in mix_peers]
-    for copy in ask:
-        copy.start()
 
     for copy in loads[1:]:
         copy.wait()
@@ -138,8 +128,27 @@
     extra = jnp.concatenate([shadow] + diagonals + [jnp.zeros((2, COV), F32)], axis=0)
     halves[0, COV:, :] = extra
     halves[1, COV:, :] = extra
+    loads[0].wait()
+    for k in range(8):
+        own[k : k + 1, :] = jnp.full((1, LANES), samp_ref[k % SAMP], jnp.int32)
+    asked[member] = own[...]
+    pl.semaphore_wait(barrier, len(Z_FAR) + len(FOUR_FAR) + len(MIX_FAR))
+
+    ask = [remote(own, asked.at[member], base + peer, z) for peer in mix_peers]
+    for copy in ask:
+        copy.start()
+
     a_core = remote(halves.at[1 - core], half_in, sibling, z)
     a_core.start()
+
+    a_core.wait_recv()
+    mine = halves[core] + half_in[...]
+    for i in range(NZ):
+        pieces[i] = jnp.concatenate([mine[i * 16 : (i + 1) * 16], mine[COV:]], axis=0)
+    piece_in[z] = pieces[z]
+    a_z = [remote(pieces.at[peer], piece_in.at[z], wide, peer) for peer in z_peers]
+    for copy in a_z:
+        copy.start()
 
     for copy in ask:
         copy.wait_recv()
@@ -173,13 +182,14 @@
     for copy in rows:
         copy.start()
 
-    a_core.wait_recv()
-    mine = halves[core] + half_in[...]
-    for i in range(NZ):
-        pieces[i] = jnp.concatenate([mine[i * 16 : (i + 1) * 16], mine[COV:]], axis=0)
-    piece_in[z] = pieces[z]
-    a_z = [remote(pieces.at[peer], piece_in.at[z], wide, peer) for peer in z_peers]
     for copy in a_z:
+        copy.wait_recv()
+    total = piece_in[0]
+    for i in range(1, NZ):
+        total = total + piece_in[i]
+    row_in[x] = total
+    a_x = [remote(row_in.at[x], row_in.at[x], peer, z) for peer in x_peers]
+    for copy in a_x:
         copy.start()
 
     for copy in rows:
@@ -196,14 +206,14 @@
     for copy in s_z:
         copy.start()
 
-    for copy in a_z:
-        copy.wait_recv()
-    total = piece_in[0]
-    for i in range(1, NZ):
-        total = total + piece_in[i]
-    row_in[x] = total
-    a_x = [remote(row_in.at[x], row_in.at[x], peer, z) for peer in x_peers]
     for copy in a_x:
+        copy.wait_recv()
+    total = row_in[0]
+    for i in range(1, NX):
+        total = total + row_in[i]
+    col_in[y] = total
+    a_y = [remote(col_in.at[y], col_in.at[y], peer, z) for peer in y_peers]
+    for copy in a_y:
         copy.start()
 
     for copy in s_z:
@@ -218,29 +228,19 @@
     for one, two in zip(s_first, s_second):
         one.start()
         two.start()
-
-    for copy in a_x:
-        copy.wait_recv()
-    total = row_in[0]
-    for i in range(1, NX):
-        total = total + row_in[i]
-    col_in[y] = total
-    a_y = [remote(col_in.at[y], col_in.at[y], peer, z) for peer in y_peers]
-    for copy in a_y:
-        copy.start()
-
-    for copy in s_first + s_second:
-        copy.wait_recv()
-    line = sketch_ref.at[0, core, y]
-    other = sketch_ref.at[1, core, x]
-    s_line = [remote(line, line, peer, z) for peer in y_peers]
-    s_other = [remote(other, other, peer, z) for peer in x_peers]
-    for one, two in zip(s_line, s_other):
-        one.start()
-        two.start()
-    s_core = [remote(line, line, sibling, z), remote(other, other, sibling, z)]
-    for copy in s_core:
-        copy.start()
+    s_line = [[] for _ in FOUR_FAR]
+    s_other = [[] for _ in FOUR_FAR]
+
+    def along(x_from, y_from):
+        line = sketch_ref.at[0, core, y, x_from]
+        other = sketch_ref.at[1, core, x, y_from]
+        for i in range(len(FOUR_FAR)):
+            s_line[i].append(remote(line, line, y_peers[i], z))
+            s_other[i].append(remote(other, other, x_peers[i], z))
+            s_line[i][-1].start()
+            s_other[i][-1].start()
+
+    along(x, y)
 
     for copy in a_y:
         copy.wait_recv()
@@ -254,13 +254,25 @@
     for copy in a_out:
         copy.start()
 
+    for i in (2, 1, 0):
+        s_first[i].wait_recv()
+        s_second[i].wait_recv()
+        along(lax.rem(x - FOUR_FAR[i] + 4, 4), lax.rem(y - FOUR_FAR[i] + 4, 4))
+    line = sketch_ref.at[0, core, y]
+    other = sketch_ref.at[1, core, x]
+    s_core = [remote(line, line, sibling, z), remote(other, other, sibling, z)]
+    for copy in s_core:
+        copy.start()
+
     def onward(index):
-        s_line[index].wait_recv()
+        for copy in s_line[index]:
+            copy.wait_recv()
         passed = sketch_ref.at[0, core, lax.rem(y - FOUR_FAR[index] + 4, 4)]
         copy = remote(passed, passed, sibling, z)
         copy.start()
         s_core.append(copy)
-        s_other[index].wait_recv()
+        for copy in s_other[index]:
+            copy.wait_recv()
         passed = sketch_ref.at[1, core, lax.rem(x - FOUR_FAR[index] + 4, 4)]
         copy = remote(passed, passed, sibling, z)
         copy.start()
@@ -277,11 +289,12 @@
     for copy in s_core:
         copy.wait_recv()
     sums = [a_core] + a_z + a_x + a_y + a_out + [a_last]
-    for copy in ask + rows + s_z + s_first + s_second + s_line + s_other + s_core + sums:
+    lines = [copy for group in s_line + s_other for copy in group]
+    for copy in ask + rows + s_z + s_first + s_second + lines + s_core + sums:
         copy.wait_send()
 
 
-N_COPIES = 7 + 1 + 7 + 7 + 7 + 3 + 6 + 3 + 6 + 8 + 7 + 1
+N_COPIES = 7 + 1 + 7 + 7 + 7 + 3 + 6 + 3 + 24 + 8 + 7 + 1
 
 
 def gather(samples, covariates, codes, bits, noise):

time: 49.1 us -> 48 us (0.978)
  Pallas kernels: 48.3 us -> 47.3 us
    pallas_call x1, Pallas kernels: 33.6 us -> 32.6 us  [gather(): pl.pallas_call(gather_kernel, out_shape=(jax.ShapeDtypeStruct((2, 2, 4, 4...]
where the time goes in v5:
time: 48 us; the launch traced here: 47.9 us
  Pallas kernels  47.3 us (99%)
  between operations  0.64 us (1%)
    pallas_call x1, Pallas kernels, gather(): pl.pallas_call(gather_kernel, out_shape=(jax.ShapeDtypeStruct((2, 2, 4, 4...  32.6 us
    pallas_call x1, Pallas kernels, solve(): pl.pallas_call(solve_kernel, out_shape=(jax.ShapeDtypeStruct((1, COLS), F...  14.7 us

profile of v5, /device:TPU:1, one launch (start us, length us, event | category | flops | bytes accessed | tf_op | source)
XLA Modules:
  0.0 47.9 jit_solution(8684833541820420049)
XLA Ops:
  0.6 32.6 %gather_sketch.1 = (bf16[2,2,4,4,16,512]{5,4,3,2,1,0:T(8,128)(2,1)S(1)}, f32[2,8,16,128]{3,2,1,0:T(8,128)S(1)}, f32[8,128]{1,0:T(8,128)S(1)}) custom-call(s32[4]{0:T(128)} %samp_hbm.1, bf16[2048,128]{1,0:T(8,128)(2,1)} %cov_hbm.3, s32[1,2048]{1,0:T(1,128)} %bitcast.10, s32[1,2048]{1,0:T(1,128)} %bitcast.14, f32[1,2048]{1,0:T(1,128)} %bitcast.12), custom_call_target="tpu_custom_call" | custom-call | tf_op jit(solution)/shard_map/gather_sketch/pallas_call | solution.py:303
  33.2 14.7 %solve.1 = (f32[1,512]{1,0:T(1,128)}, f32[1,2048]{1,0:T(1,128)}, f32[512,512]{1,0:T(8,128)}) custom-call(bf16[1024,512]{1,0:T(8,128)(2,1)S(1)} %bitcast.8, f32[2,128,128]{2,1,0:T(8,128)S(1)} %bitcast.9, f32[8,128]{1,0:T(8,128)S(1)} %get-tuple-element.11.extra_ref, f32[1,512]{1,0:T(1,128)} %bitcast.15, bf16[2048,128]{1,0:T(8,128)(2,1)} %cov_hbm.3, ...), custom_call_target="tpu_custom_call" | custom-call | tf_op jit(solution)/shard_map/solve/pallas_call | solution.py:593

commit v6 on v5

--- a/solution.py
+++ b/solution.py
@@ -42,6 +42,10 @@
     return high.astype(F32), middle.astype(F32), low.astype(F32)
 
 
+def blk(index):
+    return slice(index * COV, (index + 1) * COV)
+
+
 def ring(offset, size):
     return min(offset, size - offset)
 
@@ -56,9 +60,9 @@
 
 def gather_kernel(
     samp_hbm, cov_hbm, codes_hbm, bits_hbm, noise_hbm,
-    sketch_ref, square_ref, extra_ref,
+    gram_ref, square_ref, extra_ref,
     samp_ref, cov_ref, codes_ref, bits_ref, noise_ref,
-    own, asked, picks, lhs, sent, held, rowz,
+    own, asked, marks, picks, lhs, sent, held, rowz, sketch,
     halves, half_in, pieces, piece_in, row_in, col_in,
     send, recv, load,
 ):
@@ -128,6 +132,12 @@
     extra = jnp.concatenate([shadow] + diagonals + [jnp.zeros((2, COV), F32)], axis=0)
     halves[0, COV:, :] = extra
     halves[1, COV:, :] = extra
+    half = iota((8, LANES), 0) // SAMP
+    for chunk in range(ROWS // LANES):
+        span = slice(chunk * LANES, (chunk + 1) * LANES)
+        flips = (1 - 2 * bits_ref[:, span]).astype(F32)
+        for pair in range(2):
+            marks[pair, chunk] = jnp.where(codes_ref[:, span] == 2 * pair + half, flips, 0.0)
     loads[0].wait()
     for k in range(8):
         own[k : k + 1, :] = jnp.full((1, LANES), samp_ref[k % SAMP], jnp.int32)
@@ -160,18 +170,14 @@
     low = common ^ (common >> 1)
     top = (want >> 7) & 1
     block = want >> 8
-    upper_half = (iota(shape, 0) // SAMP) & 1
+    even = (1 - 2 * (low & 1)).astype(F32)
+    odd = even * (1 - 2 * top).astype(F32)
     for chunk in range(ROWS // LANES):
         span = slice(chunk * LANES, (chunk + 1) * LANES)
-        parity = low ^ bits_ref[:, span]
-        if chunk % 2:
-            parity = parity ^ top
-        sign = (1 - 2 * (parity & 1)).astype(F32)
-        sign = jnp.where(block == chunk // 2, sign, 0.0)
-        here = codes_ref[:, span]
+        sign = jnp.where(block == chunk // 2, odd if chunk % 2 else even, 0.0)
         for pair in range(2):
-            value = jnp.where(here == 2 * pair + upper_half, sign, 0.0)
-            picks[pair * 64 : (pair + 1) * 64, span] = value.astype(BF16)
+            value = sign.reshape(GROUP, 8, LANES) * marks[pair, chunk]
+            picks[pair * 64 : (pair + 1) * 64, span] = value.reshape(shape).astype(BF16)
     local = jnp.dot(picks[...], cov_ref[...], preferred_element_type=F32)
     local = local * (1.0 / math.sqrt(HB))
     for i in range(GROUP):
@@ -219,10 +225,10 @@
     for copy in s_z:
         copy.wait_recv()
     stack = jnp.concatenate([rowz[i].astype(F32) for i in range(NZ)], axis=0).astype(BF16)
-    sketch_ref[0, core, y, x] = stack[:16]
-    sketch_ref[1, core, x, y] = stack[16:]
-    first = sketch_ref.at[0, core, y, x]
-    second = sketch_ref.at[1, core, x, y]
+    sketch[core, 0, y, x] = stack[:16]
+    sketch[core, 1, x, y] = stack[16:]
+    first = sketch.at[core, 0, y, x]
+    second = sketch.at[core, 1, x, y]
     s_first = [remote(first, first, peer, z) for peer in x_peers]
     s_second = [remote(second, second, peer, z) for peer in y_peers]
     for one, two in zip(s_first, s_second):
@@ -232,8 +238,8 @@
     s_other = [[] for _ in FOUR_FAR]
 
     def along(x_from, y_from):
-        line = sketch_ref.at[0, core, y, x_from]
-        other = sketch_ref.at[1, core, x, y_from]
+        line = sketch.at[core, 0, y, x_from]
+        other = sketch.at[core, 1, x, y_from]
         for i in range(len(FOUR_FAR)):
             s_line[i].append(remote(line, line, y_peers[i], z))
             s_other[i].append(remote(other, other, x_peers[i], z))
@@ -258,8 +264,8 @@
         s_first[i].wait_recv()
         s_second[i].wait_recv()
         along(lax.rem(x - FOUR_FAR[i] + 4, 4), lax.rem(y - FOUR_FAR[i] + 4, 4))
-    line = sketch_ref.at[0, core, y]
-    other = sketch_ref.at[1, core, x]
+    line = sketch.at[core, 0, y]
+    other = sketch.at[core, 1, x]
     s_core = [remote(line, line, sibling, z), remote(other, other, sibling, z)]
     for copy in s_core:
         copy.start()
@@ -267,13 +273,13 @@
     def onward(index):
         for copy in s_line[index]:
             copy.wait_recv()
-        passed = sketch_ref.at[0, core, lax.rem(y - FOUR_FAR[index] + 4, 4)]
+        passed = sketch.at[core, 0, lax.rem(y - FOUR_FAR[index] + 4, 4)]
         copy = remote(passed, passed, sibling, z)
         copy.start()
         s_core.append(copy)
         for copy in s_other[index]:
             copy.wait_recv()
-        passed = sketch_ref.at[1, core, lax.rem(x - FOUR_FAR[index] + 4, 4)]
+        passed = sketch.at[core, 1, lax.rem(x - FOUR_FAR[index] + 4, 4)]
         copy = remote(passed, passed, sibling, z)
         copy.start()
         s_core.append(copy)
@@ -285,9 +291,21 @@
     a_last = remote(square_ref.at[core], square_ref.at[core], sibling, z)
     a_last.start()
     onward(0)
+
+    def gram_of(source, k):
+        rows = sketch[source].reshape(SKETCH // 2, COLS)
+        return lax.dot_general(
+            rows[:, blk(k)], rows[:, k * COV :], (((0,), (0,)), ((), ())),
+            preferred_element_type=F32,
+        )
+
+    for k in range(LEVELS):
+        gram_ref[k, :, k * COV :] = gram_of(core, k)
     a_last.wait_recv()
     for copy in s_core:
         copy.wait_recv()
+    for k in range(LEVELS):
+        gram_ref[k, :, k * COV :] = gram_ref[k, :, k * COV :] + gram_of(1 - core, k)
     sums = [a_core] + a_z + a_x + a_y + a_out + [a_last]
     lines = [copy for group in s_line + s_other for copy in group]
     for copy in ask + rows + s_z + s_first + s_second + lines + s_core + sums:
@@ -303,7 +321,7 @@
     return pl.pallas_call(
         gather_kernel,
         out_shape=(
-            jax.ShapeDtypeStruct((2, 2, 4, 4, 16, COLS), BF16),
+            jax.ShapeDtypeStruct((LEVELS, COV, COLS), F32),
             jax.ShapeDtypeStruct((2, NZ, 16, COV), F32),
             jax.ShapeDtypeStruct((EXTRA, COV), F32),
         ),
@@ -317,11 +335,13 @@
             pltpu.VMEM((1, ROWS), F32),
             pltpu.VMEM((8, LANES), jnp.int32),
             pltpu.VMEM((GROUP, 8, LANES), jnp.int32),
+            pltpu.VMEM((2, ROWS // LANES, 8, LANES), F32),
             pltpu.VMEM((2 * 64, ROWS), BF16),
             pltpu.VMEM((COLS, ROWS), BF16),
             pltpu.VMEM((GROUP, SAMP, COLS), BF16),
             pltpu.VMEM((GROUP, SAMP, COLS), BF16),
             pltpu.VMEM((NZ, SAMP, COLS), BF16),
+            pltpu.VMEM((2, 2, NY, NX, 16, COLS), BF16),
             pltpu.VMEM((2, COV + EXTRA, COV), F32),
             pltpu.VMEM((COV + EXTRA, COV), F32),
             pltpu.VMEM((NZ, 16 + EXTRA, COV), F32),
@@ -443,12 +463,8 @@
     return jnp.concatenate(rows, axis=0)
 
 
-def blk(index):
-    return slice(index * COV, (index + 1) * COV)
-
-
 def solve_kernel(
-    sketch_ref, square_ref, extra_ref, effects_hbm, cov_hbm, codes_hbm, noise_hbm,
+    given, square_ref, extra_ref, effects_hbm, cov_hbm, codes_hbm, noise_hbm,
     coef_ref, resid_ref, factor_hbm, gram, inverse,
     factor_ref, effects_ref, cov_ref, codes_ref, noise_ref, slots, load, store,
 ):
@@ -468,20 +484,16 @@
     sub = iota((COV, COV), 0)
     lane = iota((COV, COV), 1)
     scale = math.sqrt(LEVELS / SKETCH)
+    matrix = given[0, :, blk(0)]
     for k in range(n):
-        gram[k, :, k * COV :] = lax.dot_general(
-            sketch_ref[:, blk(k)], sketch_ref[:, k * COV :], (((0,), (0,)), ((), ())),
-            preferred_element_type=F32,
-        )
-    matrix = gram[0, :, blk(0)]
-    for k in range(n):
+        held = gram if k else given
         current = matrix
         corner = invert_factor(current, slots)
         inverse[k, :, blk(k)] = corner
         head = None
         if k + 1 < n:
-            head = product6(corner, gram[k, :, blk(k + 1)])
-            matrix = gram[k + 1, :, blk(k + 1)] - product6(head, head, turned=True)
+            head = product6(corner, held[k, :, blk(k + 1)])
+            matrix = held[k + 1, :, blk(k + 1)] - product6(head, head, turned=True)
         if k:
             inverse[k, :, : k * COV] = product6(corner, gram[k, :, : k * COV])
             factor_ref[blk(k), : k * COV] = jnp.zeros((COV, k * COV), F32)
@@ -491,7 +503,7 @@
         if k + 1 < n:
             factor_ref[blk(k), blk(k + 1)] = head * scale
         if k + 2 < n:
-            rest = product6(corner, gram[k, :, (k + 2) * COV :])
+            rest = product6(corner, held[k, :, (k + 2) * COV :])
             factor_ref[blk(k), (k + 2) * COV :] = rest * scale
             for i in range(k + 2, n):
                 upper[i] = rest[:, blk(i - k - 2)]
@@ -502,7 +514,7 @@
             for j in range(i, n):
                 if j > k + 1:
                     change = product6(upper[i], upper[j], turned=True)
-                    gram[i, :, blk(j)] = gram[i, :, blk(j)] - change
+                    gram[i, :, blk(j)] = held[i, :, blk(j)] - change
             change = product6(upper[i], inverse[k, :, : (k + 1) * COV], turned=True)
             if k:
                 gram[i, :, : k * COV] = gram[i, :, : k * COV] - change[:, : k * COV]
@@ -587,7 +599,7 @@
         copy.wait()
 
 
-def solve(sketch, square, extra, effects, covariates, codes, noise):
+def solve(gram, square, extra, effects, covariates, codes, noise):
     vmem = pl.BlockSpec(memory_space=pltpu.VMEM)
     hbm = pl.BlockSpec(memory_space=pltpu.HBM)
     return pl.pallas_call(
@@ -613,7 +625,7 @@
         ],
         compiler_params=pltpu.CompilerParams(vmem_limit_bytes=40 << 20),
         name="solve",
-    )(sketch, square, extra, effects, covariates, codes, noise)
+    )(gram, square, extra, effects, covariates, codes, noise)
 
 
 def body(covariates, level_codes, sign_bits, sample_rows, effects, noise):
@@ -623,11 +635,11 @@
     covariates = fixed(covariates)
     codes = fixed(level_codes.reshape(1, ROWS))
     noise = fixed(noise.reshape(1, ROWS))
-    sketch, square, extra = gather(
+    gram, square, extra = gather(
         fixed(sample_rows), covariates, codes, fixed(sign_bits.reshape(1, ROWS)), noise
     )
     coef, resid, factor = solve(
-        sketch.reshape(SKETCH, COLS), square.reshape(2, COV, COV), extra,
+        gram, square.reshape(2, COV, COV), extra,
         fixed(effects.reshape(1, COLS)), covariates, codes, noise,
     )
     return coef.reshape(COLS), resid.reshape(ROWS), factor

time: 48 us -> 48.5 us (1.010)
    pallas_call x1, Pallas kernels: 32.6 us -> 33.1 us  [gather(): pl.pallas_call(gather_kernel, out_shape=(jax.ShapeDtypeStruct((LEVELS, CO...]
where the time goes in v6:
time: 48.5 us; the launch traced here: 48.4 us
  Pallas kernels  47.6 us (98%)
  between operations  0.8 us (2%)
    pallas_call x1, Pallas kernels, gather(): pl.pallas_call(gather_kernel, out_shape=(jax.ShapeDtypeStruct((LEVELS, CO...  33.1 us
    pallas_call x1, Pallas kernels, solve(): pl.pallas_call(solve_kernel, out_shape=(jax.ShapeDtypeStruct((1, COLS), F...  14.5 us

profile of v6, /device:TPU:1, one launch (start us, length us, event | category | flops | bytes accessed | tf_op | source)
XLA Modules:
  0.0 48.4 jit_solution(16239702662252304602)
XLA Ops:
  0.6 33.1 %gather_sketch.1 = (f32[4,128,512]{2,1,0:T(8,128)S(1)}, f32[2,8,16,128]{3,2,1,0:T(8,128)S(1)}, f32[8,128]{1,0:T(8,128)S(1)}) custom-call(s32[4]{0:T(128)} %samp_hbm.1, bf16[2048,128]{1,0:T(8,128)(2,1)} %cov_hbm.3, s32[1,2048]{1,0:T(1,128)} %bitcast.8, s32[1,2048]{1,0:T(1,128)} %bitcast.12, f32[1,2048]{1,0:T(1,128)} %bitcast.10), custom_call_target="tpu_custom_call" | custom-call | tf_op jit(solution)/shard_map/gather_sketch/pallas_call | solution.py:321
  33.8 14.5 %solve.1 = (f32[1,512]{1,0:T(1,128)}, f32[1,2048]{1,0:T(1,128)}, f32[512,512]{1,0:T(8,128)}) custom-call(f32[4,128,512]{2,1,0:T(8,128)S(1)} %get-tuple-element.9.given, f32[2,128,128]{2,1,0:T(8,128)S(1)} %bitcast.7, f32[8,128]{1,0:T(8,128)S(1)} %get-tuple-element.11.extra_ref, f32[1,512]{1,0:T(1,128)} %bitcast.13, bf16[2048,128]{1,0:T(8,128)(2,1)} %cov_hbm.3, ...), custom_call_target="tpu_custom_call" | custom-call | tf_op jit(solution)/shard_map/solve/pallas_call | solution.py:605
